TPU v7x, 512 devices: a whole 4x8x8 slice. The times are simulated.
512 devices in a mesh: shard: 64 (over x, z, core), tensor: 8 (over y).
Axes of the slice: x: 4, y: 8, z: 8, core: 2. Of those that a mesh axis runs over, the one named last changes fastest.
Arguments:
- grad: float32 [8, 512, 1024], P(None, 'shard', 'tensor'), may hold values from -500 to 500
- momentum: float32 [8, 512, 1024], P(None, 'shard', 'tensor'), may hold values from -6 to 6
- weight: float32 [8, 512, 1024], P(None, 'shard', 'tensor'), may hold values from -0.625 to 0.625
Outputs:
- new_weight: float32 [8, 512, 1024], P(None, 'shard', 'tensor')
- new_momentum: float32 [8, 512, 1024], P(None, 'shard', 'tensor')
- update: float32 [8, 512, 1024], P(None, 'shard', 'tensor')
All inputs are finite; a program needn't handle non-finite values.
Results may differ from a plain program's by a relative error of at most 0.0078.
Values may be sent and summed in bfloat16 or wider, within the bound.
A program may use at most 64 MiB of HBM per device.

v0:
```python
import math

import jax
import jax.numpy as jnp
from jax import lax
from jax.sharding import PartitionSpec as P

ITERS = 3


mu_decay = 0.95
learn_rate = 0.05
weight_decay = 0.1
update_gain = 0.2
first_coef = 3.4445
second_coef = -4.775
third_coef = 2.0315
epsilon = 1e-07


def regroup(values):
    return lax.all_to_all(
        lax.all_to_all(values, "shard", split_axis=3, concat_axis=1, tiled=True),
        "tensor",
        split_axis=0,
        concat_axis=2,
        tiled=True,
    )


def polish(iterate, gram):
    wide = iterate.astype(jnp.float32)
    squared = jnp.einsum("mrs,mst->mrt", gram, gram, precision=lax.Precision.HIGHEST)
    poly = second_coef * gram + third_coef * squared
    mixed = jnp.einsum("mrs,msc->mrc", poly, wide, precision=lax.Precision.HIGHEST)
    fresh = first_coef * wide + mixed
    return fresh.astype(jnp.bfloat16)


def on_device(grad, momentum, weight):
    mats, rows_local, cols_local = grad.shape
    n_shard = lax.axis_size("shard")
    n_tensor = lax.axis_size("tensor")
    new_momentum = mu_decay * momentum + grad
    advance = lax.optimization_barrier((grad + mu_decay * new_momentum).astype(jnp.bfloat16))
    wide = advance.astype(jnp.float32)
    total = lax.psum(jnp.sum(wide * wide, axis=(1, 2)), ("shard", "tensor"))
    frob = jnp.sqrt(total)[:, None, None] + epsilon
    start = (wide / frob).astype(jnp.bfloat16)
    moved = regroup(start.reshape(mats, rows_local, 1, cols_local))
    group, kv_rows, tensor_cols, thin_cols = moved.shape
    gathered = lax.all_gather(moved, "shard", axis=3, tiled=True)
    iterate = gathered.reshape(group, kv_rows, tensor_cols * n_shard * thin_cols)
    for step in range(ITERS):
        gram = jnp.einsum("mrc,msc->mrs", iterate, iterate, preferred_element_type=jnp.float32)
        iterate = polish(iterate, gram)
    spread = iterate.reshape(group, kv_rows, tensor_cols, n_shard, thin_cols)
    result = lax.dynamic_index_in_dim(spread, lax.axis_index("shard"), 3, keepdims=False)
    back = lax.all_to_all(
        lax.all_to_all(result, "shard", split_axis=1, concat_axis=3, tiled=True),
        "tensor",
        split_axis=2,
        concat_axis=0,
        tiled=True,
    )
    ortho = back.reshape(mats, rows_local, cols_local)
    width = cols_local * n_tensor
    update = update_gain * math.sqrt(width) * ortho.astype(jnp.float32)
    new_weight = weight - learn_rate * (update + weight_decay * weight)
    return (new_weight, new_momentum, update)


def solution(mesh):
    in_specs = (P(None, "shard", "tensor"), P(None, "shard", "tensor"), P(None, "shard", "tensor"))
    out_specs = (P(None, "shard", "tensor"), P(None, "shard", "tensor"), P(None, "shard", "tensor"))
    return jax.shard_map(
        on_device, mesh=mesh, in_specs=in_specs, out_specs=out_specs, check_vma=False
    )
```

profile of v0, /device:TPU:1, one launch (start us, length us, event | category | flops | bytes accessed | tf_op | source)
XLA Modules:
  0.0 277.7 jit_solution(15786168088153653814)
XLA Ops:
  7.2 0.0 all-gather.3.cloned.1.call-start
  7.2 1.4 add_convert_fusion.3
  8.6 0.1 fusion.4
  8.7 106.1 %psum.7 = f32[8]{0:T(128)S(1)} all-reduce(f32[8]{0:T(128)S(1)} %fusion.4), channel_id=1, replica_groups=mesh['shard'=64,'tensor'=8] {'shard','tensor'}, use_global_device_ids=true, to_apply=%region_1.0 | all-reduce | flops 8 | bytes 64 | tf_op jit(solution)/shard_map/psum | solution.py:47
  114.8 0.1 fusion.6
  114.9 0.2 copy.53
  115.1 16.0 %all_to_all.63 = bf16[8,8,1,128]{1,0,2,3:T(8,128)(2,1)S(1)} all-to-all(bf16[8,8,1,128]{1,0,2,3:T(8,128)(2,1)S(1)} %copy.53), channel_id=1, replica_groups=mesh['shard'=64,'tensor'=8] {'shard'}, dimensions={3} | all-to-all | bytes 32768 | tf_op jit(solution)/shard_map/all_to_all | solution.py:23
  131.2 0.1 copy.66
  131.2 0.3 reshape.105
  131.5 11.5 %all_to_all.64 = bf16[8,512,1,2]{1,3,2,0:T(2,128)(2,1)S(1)} all-to-all(bf16[8,512,1,2]{1,3,2,0:T(2,128)(2,1)S(1)} %reshape.105), channel_id=1, replica_groups=mesh['shard'=64,'tensor'=8] {'tensor'}, dimensions={0} | all-to-all | bytes 32768 | tf_op jit(solution)/shard_map/all_to_all | solution.py:22
  143.0 0.6 copy.56
  143.6 0.0 all-gather.3.cloned.1.call-update
  143.7 76.4 %all-gather.3.cloned.1.call-done = bf16[1,512,8,1,128]{1,2,3,0,4:T(8,128)(2,1)} async-done(((bf16[1,512,8,1,2]{1,2,3,0,4:T(8,128)(2,1)}), bf16[1,512,8,1,128]{1,2,3,0,4:T(8,128)(2,1)}) %all-gather.3.cloned.1.call-update) | async-done | bytes 1048592 | tf_op jit(solution)/shard_map/all_gather | solution.py:52
  220.1 1.9 copy.59
  222.0 0.7 convolution_bitcast_fusion
  222.8 0.0 copy-start
  222.8 1.9 fusion.2
  224.7 0.0 copy-done
  224.7 0.3 copy.57
  225.0 0.7 copy.58
  225.7 1.9 add_convert_fusion.2
  227.6 0.7 fusion.7
  228.3 1.9 fusion.1
  230.2 1.9 add_convert_fusion.1
  232.1 0.7 fusion.8
  232.9 1.9 fusion
  234.8 1.9 add_convert_fusion
  236.6 0.5 copy.60
  237.2 0.4 reshape.100
  237.7 0.0 copy-start.1
  237.7 0.2 copy.62
  237.9 18.4 %all_to_all.65 = bf16[1,512,8,2]{2,3,0,1:T(2,128)(2,1)S(1)} all-to-all(bf16[1,512,8,2]{2,3,0,1:T(2,128)(2,1)S(1)} %copy.62), channel_id=1, replica_groups=mesh['shard'=64,'tensor'=8] {'shard'}, dimensions={1} | all-to-all | bytes 32768 | tf_op jit(solution)/shard_map/all_to_all | solution.py:60
  256.3 0.5 copy.69
  256.8 0.4 copy.64
  257.2 0.2 copy.65
  257.4 12.9 %all_to_all.66 = bf16[1,8,8,128]{3,1,0,2:T(8,128)(2,1)S(1)} all-to-all(bf16[1,8,8,128]{3,1,0,2:T(8,128)(2,1)S(1)} %copy.65), channel_id=1, replica_groups=mesh['shard'=64,'tensor'=8] {'tensor'}, dimensions={2} | all-to-all | bytes 32768 | tf_op jit(solution)/shard_map/all_to_all | solution.py:59
  270.2 0.0 copy-done.1
  270.2 0.6 multiply_subtract_fusion
  (2 shorter events, 0.0 us)
Async XLA Ops:
  7.2 212.9 %all-gather.3.cloned.1.call-start = ((), (), s32[]{:S(2)}) async-start(), calls=%async_computation.4 | async-start | bytes 1064960 | tf_op jit(solution)/shard_map/all_gather | solution.py:52
  222.8 1.9 copy-start
  237.7 32.5 %copy-start.1 = (f32[8,8,128]{2,1,0:T(8,128)S(1)}, f32[8,8,128]{2,1,0:T(8,128)}, u32[]{:S(2)}) copy-start(f32[8,8,128]{2,1,0:T(8,128)} %param.5) | copy-start | bytes 98308
Sparse Core Ops, SparseCore 0:
  143.8 76.2 all-gather.2
where the time goes:
time: 278 us
  blocking collectives  165 us (59%)
  waiting for transfers between devices  76.4 us (27%)
  between operations  14.2 us (5%)
  matrix products  13.5 us (5%)
  local copies, waits for them, and re-layouts  6.34 us (2%)
    psum x1, blocking collectives, on_device(): total = lax.psum(jnp.sum(wide * wide, axis=(1, 2)), ('shard', 'tensor'))  106 us
    all_gather x1, waiting for transfers between devices, on_device(): gathered = lax.all_gather(moved, 'shard', axis=3, tiled=True)  76.4 us
    all_to_all x1, blocking collectives, on_device(): lax.all_to_all(result, 'shard', split_axis=1, concat_axis=3, tiled=True)  18.4 us
    all_to_all x1, blocking collectives, regroup(): lax.all_to_all(values, 'shard', split_axis=3, concat_axis=1, tiled=True)  16 us
    all_to_all x1, blocking collectives, on_device(): lax.all_to_all(lax.all_to_all(result, 'shard', split_axis=1, concat_axis=...  12.9 us
    all_to_all x1, blocking collectives, regroup(): lax.all_to_all(lax.all_to_all(values, 'shard', split_axis=3, concat_axis=...  11.5 us
    dot_general x3, matrix products, polish(): jnp.einsum('mrs,mst->mrt', gram, gram, precision=lax.Precision.HIGHEST)  5.7 us
    dot_general x3, matrix products, polish(): jnp.einsum('mrs,msc->mrc', poly, wide, precision=lax.Precision.HIGHEST)  5.59 us
  transfers between devices with their start and end apart: 1, of which 1 were waited for; matrix products, arithmetic and copies ran while one was open for 0% of the time, Pallas kernels for 0%

commit v1 on v0

v1 whole, which is shorter than its diff:
```python
import math

import jax
import jax.numpy as jnp
from jax import lax
from jax.sharding import PartitionSpec as P

ITERS = 3


mu_decay = 0.95
learn_rate = 0.05
weight_decay = 0.1
update_gain = 0.2
first_coef = 3.4445
second_coef = -4.775
third_coef = 2.0315
epsilon = 1e-07


def polish(iterate, gram):
    wide = iterate.astype(jnp.float32)
    squared = jnp.dot(gram, gram, precision=lax.Precision.HIGHEST)
    poly = second_coef * gram + third_coef * squared
    mixed = jnp.dot(poly, wide, precision=lax.Precision.HIGHEST)
    fresh = first_coef * wide + mixed
    return fresh.astype(jnp.bfloat16)


def on_device(grad, momentum, weight):
    mats, rows_local, cols_local = grad.shape
    n_tensor = lax.axis_size("tensor")
    new_momentum = mu_decay * momentum + grad
    advance = (grad + mu_decay * new_momentum).astype(jnp.bfloat16)
    mine = lax.all_to_all(advance, "tensor", split_axis=0, concat_axis=2, tiled=True)
    whole = lax.all_gather(mine, "shard", axis=1, tiled=True)[0]
    wide = whole.astype(jnp.float32)
    frob = jnp.sqrt(jnp.sum(wide * wide)) + epsilon
    iterate = (wide / frob).astype(jnp.bfloat16)
    for step in range(ITERS):
        gram = jnp.dot(iterate, iterate.T, preferred_element_type=jnp.float32)
        iterate = polish(iterate, gram)
    start = lax.axis_index("shard") * rows_local
    rows = lax.dynamic_slice_in_dim(iterate, start, rows_local, axis=0)
    ortho = lax.all_to_all(rows[None], "tensor", split_axis=2, concat_axis=0, tiled=True)
    width = cols_local * n_tensor
    update = update_gain * math.sqrt(width) * ortho.astype(jnp.float32)
    new_weight = weight - learn_rate * (update + weight_decay * weight)
    return (new_weight, new_momentum, update)


def solution(mesh):
    in_specs = (P(None, "shard", "tensor"), P(None, "shard", "tensor"), P(None, "shard", "tensor"))
    out_specs = (P(None, "shard", "tensor"), P(None, "shard", "tensor"), P(None, "shard", "tensor"))
    return jax.shard_map(
        on_device, mesh=mesh, in_specs=in_specs, out_specs=out_specs, check_vma=False
    )
```

time: 278 us -> 151 us (0.54)
  blocking collectives: 165 us -> 27 us
  waiting for transfers between devices: 76.4 us -> 84.4 us
  other arithmetic: 2.27 us -> 7.41 us
  local copies, waits for them, and re-layouts: 6.34 us -> 2.04 us
    psum x1 -> x0, blocking collectives: 106 us -> none  [on_device(): total = lax.psum(jnp.sum(wide * wide, axis=(1, 2)), ('shard', 'tensor'))]
    all_to_all x4 -> x2, blocking collectives: 58.8 us -> 27 us  [the longest x1 14.2 us: on_device(): lax.all_to_all(advance, 'tensor', split_axis=0, concat_axis=2, tiled=True)]
    all_gather x1, waiting for transfers between devices: 76.4 us -> 84.4 us  [on_device(): whole = lax.all_gather(mine, 'shard', axis=1, tiled=True)[0]]
where the time goes in v1:
time: 151 us
  waiting for transfers between devices  84.4 us (56%)
  blocking collectives  27 us (18%)
  matrix products  15.3 us (10%)
  between operations  14.9 us (10%)
  other arithmetic  7.41 us (5%)
  local copies, waits for them, and re-layouts  2.04 us (1%)
    all_gather x1, waiting for transfers between devices, on_device(): whole = lax.all_gather(mine, 'shard', axis=1, tiled=True)[0]  84.4 us
    all_to_all x1, blocking collectives, on_device(): lax.all_to_all(advance, 'tensor', split_axis=0, concat_axis=2, tiled=True)  14.2 us
    all_to_all x1, blocking collectives, on_device(): lax.all_to_all(rows[None], 'tensor', split_axis=2, concat_axis=0, tiled=T...  12.9 us
    dot_general x3, matrix products, polish(): mixed = jnp.dot(poly, wide, precision=lax.Precision.HIGHEST)  5.81 us
    dot_general x3, matrix products, polish(): squared = jnp.dot(gram, gram, precision=lax.Precision.HIGHEST)  5.73 us
    dot_general x3, matrix products, on_device(): gram = jnp.dot(iterate, iterate.T, preferred_element_type=jnp.float32)  3.78 us
  transfers between devices with their start and end apart: 1, of which 1 were waited for; matrix products, arithmetic and copies ran while one was open for 0% of the time, Pallas kernels for 0%

profile of v1, /device:TPU:1, one launch (start us, length us, event | category | flops | bytes accessed | tf_op | source)
XLA Modules:
  0.0 151.1 jit_solution(5558221943511022706)
XLA Ops:
  7.2 0.0 all-gather.2.cloned.1.call-start
  7.2 1.4 add_convert_fusion.2
  8.6 14.2 %all_to_all.27 = bf16[8,8,128]{2,1,0:T(8,128)(2,1)} all-to-all(bf16[8,8,128]{2,1,0:T(8,128)(2,1)S(1)} %get-tuple-element.3), channel_id=1, replica_groups=mesh['shard'=64,'tensor'=8] {'tensor'}, dimensions={0} | all-to-all | bytes 32768 | tf_op jit(solution)/shard_map/all_to_all | solution.py:35
  22.8 0.0 all-gather.2.cloned.1.call-update
  22.8 84.4 %all-gather.2.cloned.1.call-done = bf16[1,512,1024]{2,1,0:T(8,128)(2,1)} async-done(((bf16[1,8,1024]{2,1,0:T(8,128)(2,1)}), bf16[1,512,1024]{2,1,0:T(8,128)(2,1)}) %all-gather.2.cloned.1.call-update) | async-done | bytes 1048592 | tf_op jit(solution)/shard_map/all_gather | solution.py:36
  107.2 2.4 %fusion = f32[]{:T(128)} fusion(bf16[1,512,1024]{2,1,0:T(8,128)(2,1)} %all-gather.2.cloned.1.call-done), kind=kLoop, calls=%fused_computation.2 | loop fusion | flops 1572863 | bytes 1048580 | tf_op jit(solution)/shard_map/reduce_sum | solution.py:38
  110.2 2.3 %fusion.8 = f32[512,512]{1,0:T(8,128)S(1)} fusion(bf16[1,512,1024]{2,1,0:T(8,128)(2,1)} %all-gather.2.cloned.1.call-done, f32[]{:T(128)S(6)} %add.35), kind=kOutput, calls=%fused_computation.20 | convolution fusion | flops 538443776 | bytes 2097156 | tf_op jit(solution)/shard_map/dot_general | solution.py:41
  112.5 0.0 copy-start
  112.5 1.9 %fusion.4 = f32[512,512]{1,0:T(8,128)S(1)} fusion(f32[512,512]{1,0:T(8,128)S(1)} %fusion.8), kind=kOutput, calls=%fused_computation.11 | convolution fusion | flops 1611399168 | bytes 2097152 | tf_op jit(solution)/shard_map/dot_general | solution.py:23
  114.5 0.0 copy-done
  114.5 1.9 %add_convert_fusion.1 = bf16[512,1024]{1,0:T(8,128)(2,1)S(1)} fusion(f32[512,512]{1,0:T(8,128)S(1)} %fusion.4, f32[]{:T(128)S(6)} %add.35, bf16[1,512,1024]{2,1,0:T(8,128)(2,1)S(1)} %copy-done), kind=kOutput, calls=%fused_computation.5 | convolution fusion | flops 3226468352 | bytes 3145732 | tf_op jit(solution)/shard_map/dot_general | solution.py:25
  116.4 0.7 fusion.11
  117.1 1.9 %fusion.3 = f32[512,512]{1,0:T(8,128)S(1)} fusion(f32[512,512]{1,0:T(8,128)S(1)} %fusion.11), kind=kOutput, calls=%fused_computation.9 | convolution fusion | flops 1611399168 | bytes 2097152 | tf_op jit(solution)/shard_map/dot_general | solution.py:23
  119.1 1.9 %add_convert_fusion = bf16[512,1024]{1,0:T(8,128)(2,1)S(1)} fusion(bf16[512,1024]{1,0:T(8,128)(2,1)S(1)} %add_convert_fusion.1, f32[512,512]{1,0:T(8,128)S(1)} %fusion.3), kind=kOutput, calls=%fused_computation.4 | convolution fusion | flops 3223322624 | bytes 3145728 | tf_op jit(solution)/shard_map/dot_general | solution.py:25
  120.9 0.7 fusion.12
  121.7 1.9 %fusion.2 = f32[512,512]{1,0:T(8,128)S(1)} fusion(f32[512,512]{1,0:T(8,128)S(1)} %fusion.12), kind=kOutput, calls=%fused_computation.7 | convolution fusion | flops 1611399168 | bytes 2097152 | tf_op jit(solution)/shard_map/dot_general | solution.py:23
  123.6 2.0 %fusion.13 = f32[512,1024]{1,0:T(8,128)S(1)} fusion(f32[512,512]{1,0:T(8,128)S(1)} %fusion.2, bf16[512,1024]{1,0:T(8,128)(2,1)S(1)} %add_convert_fusion), kind=kOutput, calls=%fused_computation.23 | convolution fusion | flops 3221225472 | bytes 4194304 | tf_op jit(solution)/shard_map/dot_general | solution.py:25
  125.6 0.0 copy-start.2
  125.7 0.4 copy.7
  126.1 0.5 broadcast.39
  126.6 2.3 %reduce.1 = bf16[1024,8]{1,0:T(8,128)(2,1)S(1)} reduce(bf16[1024,1,8]{2,1,0:T(2,128)(2,1)S(1)} %bitcast.37, bf16[]{:T(256)} %broadcast.39), dimensions={1}, to_apply=%bitcast.18.reduce_sub_computation | reduce | bytes 32770
  128.8 0.3 reshape.19
  129.1 12.9 %all_to_all.28 = bf16[8,2,512]{2,1,0:T(2,128)(2,1)S(1)} all-to-all(bf16[8,2,512]{2,1,0:T(2,128)(2,1)S(1)} %reshape.19), channel_id=1, replica_groups=mesh['shard'=64,'tensor'=8] {'tensor'}, dimensions={0} | all-to-all | bytes 32768 | tf_op jit(solution)/shard_map/all_to_all | solution.py:45
  142.0 0.7 reshape.20
  142.7 0.7 convert_multiply_fusion.1
  143.4 0.2 copy.8
  143.6 0.0 copy-done.2
  143.6 0.0 copy-start.1
  143.6 0.6 multiply_subtract_fusion
  144.2 0.0 copy-done.1
  (1 shorter events, 0.0 us)
Async XLA Ops:
  7.2 100.0 %all-gather.2.cloned.1.call-start = ((), (), s32[]{:S(2)}) async-start(), calls=%async_computation.2 | async-start | bytes 1064960 | tf_op jit(solution)/shard_map/all_gather | solution.py:36
  112.5 1.9 %copy-start = (bf16[1,512,1024]{2,1,0:T(8,128)(2,1)S(1)}, bf16[1,512,1024]{2,1,0:T(8,128)(2,1)}, u32[]{:S(2)}) copy-start(bf16[1,512,1024]{2,1,0:T(8,128)(2,1)} %all-gather.2.cloned.1.call-done) | copy-start | bytes 3145732
  125.6 18.0 %copy-start.2 = (f32[8,8,128]{2,1,0:T(8,128)S(1)}, f32[8,8,128]{2,1,0:T(8,128)}, u32[]{:S(2)}) copy-start(f32[8,8,128]{2,1,0:T(8,128)} %param.5) | copy-start | bytes 98308
  143.6 0.6 copy-start.1
Sparse Core Ops, SparseCore 0:
  22.9 84.2 all-gather.1

commit v2 on v1

--- a/solution.py
+++ b/solution.py
@@ -6,6 +6,7 @@
 from jax.sharding import PartitionSpec as P
 
 ITERS = 3
+SHARD_AXES = ("sx", "sz", "sc")
 
 
 mu_decay = 0.95
@@ -33,14 +34,19 @@
     new_momentum = mu_decay * momentum + grad
     advance = (grad + mu_decay * new_momentum).astype(jnp.bfloat16)
     mine = lax.all_to_all(advance, "tensor", split_axis=0, concat_axis=2, tiled=True)
-    whole = lax.all_gather(mine, "shard", axis=1, tiled=True)[0]
+    for axis in SHARD_AXES:
+        mine = lax.all_gather(mine, axis, axis=1, tiled=True)
+    whole = mine[0]
     wide = whole.astype(jnp.float32)
     frob = jnp.sqrt(jnp.sum(wide * wide)) + epsilon
     iterate = (wide / frob).astype(jnp.bfloat16)
     for step in range(ITERS):
         gram = jnp.dot(iterate, iterate.T, preferred_element_type=jnp.float32)
         iterate = polish(iterate, gram)
-    start = lax.axis_index("shard") * rows_local
+    block = 0
+    for axis in reversed(SHARD_AXES):
+        block = block * lax.axis_size(axis) + lax.axis_index(axis)
+    start = block * rows_local
     rows = lax.dynamic_slice_in_dim(iterate, start, rows_local, axis=0)
     ortho = lax.all_to_all(rows[None], "tensor", split_axis=2, concat_axis=0, tiled=True)
     width = cols_local * n_tensor
@@ -49,9 +55,24 @@
     return (new_weight, new_momentum, update)
 
 
+def split_shard(mesh):
+    devices = mesh.devices
+    column = devices[:, 0]
+    try:
+        n_x = len({d.coords[0] for d in column})
+        n_z = len({d.coords[2] for d in column})
+        n_core = len({d.core_on_chip for d in column})
+    except AttributeError:
+        n_x, n_z, n_core = len(column), 1, 1
+    if n_x * n_z * n_core != len(column):
+        n_x, n_z, n_core = len(column), 1, 1
+    grid = devices.reshape(n_x, n_z, n_core, devices.shape[1])
+    return jax.sharding.Mesh(grid, SHARD_AXES + ("tensor",))
+
+
 def solution(mesh):
-    in_specs = (P(None, "shard", "tensor"), P(None, "shard", "tensor"), P(None, "shard", "tensor"))
-    out_specs = (P(None, "shard", "tensor"), P(None, "shard", "tensor"), P(None, "shard", "tensor"))
+    fine = split_shard(mesh)
+    spec = P(None, SHARD_AXES, "tensor")
     return jax.shard_map(
-        on_device, mesh=mesh, in_specs=in_specs, out_specs=out_specs, check_vma=False
+        on_device, mesh=fine, in_specs=(spec,) * 3, out_specs=(spec,) * 3, check_vma=False
     )

time: 151 us -> 125 us (0.83)
  waiting for transfers between devices: 84.4 us -> 21.1 us
  blocking collectives: 27 us -> 63.7 us
    all_gather x1, waiting for transfers between devices: 84.4 us -> 21.1 us  [on_device(): mine = lax.all_gather(mine, axis, axis=1, tiled=True)]
    all_gather x0 -> x2, blocking collectives: none -> 37.8 us  [on_device(): mine = lax.all_gather(mine, axis, axis=1, tiled=True)]
where the time goes in v2:
time: 125 us
  blocking collectives  63.7 us (51%)
  waiting for transfers between devices  21.1 us (17%)
  matrix products  15.3 us (12%)
  between operations  14.9 us (12%)
  other arithmetic  7.41 us (6%)
  local copies, waits for them, and re-layouts  2.04 us (2%)
    all_gather x2, blocking collectives, on_device(): mine = lax.all_gather(mine, axis, axis=1, tiled=True)  37.8 us
    all_gather x1, waiting for transfers between devices, on_device(): mine = lax.all_gather(mine, axis, axis=1, tiled=True)  21.1 us
    all_to_all x1, blocking collectives, on_device(): lax.all_to_all(advance, 'tensor', split_axis=0, concat_axis=2, tiled=True)  14 us
    all_to_all x1, blocking collectives, on_device(): lax.all_to_all(rows[None], 'tensor', split_axis=2, concat_axis=0, tiled=T...  11.9 us
    dot_general x3, matrix products, polish(): mixed = jnp.dot(poly, wide, precision=lax.Precision.HIGHEST)  5.81 us
    dot_general x3, matrix products, polish(): squared = jnp.dot(gram, gram, precision=lax.Precision.HIGHEST)  5.73 us
    dot_general x3, matrix products, on_device(): gram = jnp.dot(iterate, iterate.T, preferred_element_type=jnp.float32)  3.78 us
  transfers between devices with their start and end apart: 1, of which 1 were waited for; matrix products, arithmetic and copies ran while one was open for 0% of the time, Pallas kernels for 0%

profile of v2, /device:TPU:1, one launch (start us, length us, event | category | flops | bytes accessed | tf_op | source)
XLA Modules:
  0.0 124.5 jit_solution(15366829730807297740)
XLA Ops:
  7.2 0.0 all-gather.2.cloned.1.call-start
  7.2 1.4 %add_convert_fusion.2 = (bf16[8,8,128]{2,1,0:T(8,128)(2,1)S(1)}, f32[8,8,128]{2,1,0:T(8,128)}) fusion(f32[8,8,128]{2,1,0:T(8,128)} %param.3, f32[8,8,128]{2,1,0:T(8,128)} %param.4), kind=kLoop, calls=%fused_computation.17 | loop fusion | flops 40960 | bytes 114688 | tf_op jit(solution)/shard_map/convert_element_type | solution.py:35
  8.6 14.0 %all_to_all.27 = bf16[8,8,128]{2,1,0:T(8,128)(2,1)S(1)} all-to-all(bf16[8,8,128]{2,1,0:T(8,128)(2,1)S(1)} %get-tuple-element.3), channel_id=1, replica_groups=mesh['sx'=4,'sz'=8,'sc'=2,'tensor'=8] {'tensor'}, dimensions={0} | all-to-all | bytes 32768 | tf_op jit(solution)/shard_map/all_to_all | solution.py:36
  22.7 9.3 %all_gather.9 = bf16[1,32,1024]{2,1,0:T(8,128)(2,1)S(1)} all-gather(bf16[1,8,1024]{2,1,0:T(8,128)(2,1)S(1)} %bitcast.40), channel_id=1, replica_groups=mesh['sx'=4,'sz'=8,'sc'=2,'tensor'=8] {'sx'}, dimensions={1}, use_global_device_ids=true | all-gather | bytes 81920 | tf_op jit(solution)/shard_map/all_gather | solution.py:38
  32.0 28.4 %all_gather.10 = bf16[1,256,1024]{2,1,0:T(8,128)(2,1)} all-gather(bf16[1,32,1024]{2,1,0:T(8,128)(2,1)S(1)} %all_gather.9), channel_id=1, replica_groups=mesh['sx'=4,'sz'=8,'sc'=2,'tensor'=8] {'sz'}, dimensions={1}, use_global_device_ids=true | all-gather | bytes 589824 | tf_op jit(solution)/shard_map/all_gather | solution.py:38
  60.4 0.0 all-gather.2.cloned.1.call-update
  60.4 21.1 %all-gather.2.cloned.1.call-done = bf16[1,512,1024]{2,1,0:T(8,128)(2,1)} async-done(((bf16[1,256,1024]{2,1,0:T(8,128)(2,1)}), bf16[1,512,1024]{2,1,0:T(8,128)(2,1)}) %all-gather.2.cloned.1.call-update) | async-done | bytes 1048592 | tf_op jit(solution)/shard_map/all_gather | solution.py:38
  81.6 2.4 %fusion = f32[]{:T(128)} fusion(bf16[1,512,1024]{2,1,0:T(8,128)(2,1)} %all-gather.2.cloned.1.call-done), kind=kLoop, calls=%fused_computation.2 | loop fusion | flops 1572863 | bytes 1048580 | tf_op jit(solution)/shard_map/reduce_sum | solution.py:41
  84.6 2.3 %fusion.8 = f32[512,512]{1,0:T(8,128)S(1)} fusion(bf16[1,512,1024]{2,1,0:T(8,128)(2,1)} %all-gather.2.cloned.1.call-done, f32[]{:T(128)S(6)} %add.41), kind=kOutput, calls=%fused_computation.20 | convolution fusion | flops 538443776 | bytes 2097156 | tf_op jit(solution)/shard_map/dot_general | solution.py:44
  86.9 0.0 copy-start
  86.9 1.9 %fusion.4 = f32[512,512]{1,0:T(8,128)S(1)} fusion(f32[512,512]{1,0:T(8,128)S(1)} %fusion.8), kind=kOutput, calls=%fused_computation.11 | convolution fusion | flops 1611399168 | bytes 2097152 | tf_op jit(solution)/shard_map/dot_general | solution.py:24
  88.9 0.0 copy-done
  88.9 1.9 %add_convert_fusion.1 = bf16[512,1024]{1,0:T(8,128)(2,1)S(1)} fusion(f32[512,512]{1,0:T(8,128)S(1)} %fusion.4, f32[]{:T(128)S(6)} %add.41, bf16[1,512,1024]{2,1,0:T(8,128)(2,1)S(1)} %copy-done), kind=kOutput, calls=%fused_computation.5 | convolution fusion | flops 3226468352 | bytes 3145732 | tf_op jit(solution)/shard_map/dot_general | solution.py:26
  90.8 0.7 fusion.11
  91.5 1.9 %fusion.3 = f32[512,512]{1,0:T(8,128)S(1)} fusion(f32[512,512]{1,0:T(8,128)S(1)} %fusion.11), kind=kOutput, calls=%fused_computation.9 | convolution fusion | flops 1611399168 | bytes 2097152 | tf_op jit(solution)/shard_map/dot_general | solution.py:24
  93.5 1.9 %add_convert_fusion = bf16[512,1024]{1,0:T(8,128)(2,1)S(1)} fusion(bf16[512,1024]{1,0:T(8,128)(2,1)S(1)} %add_convert_fusion.1, f32[512,512]{1,0:T(8,128)S(1)} %fusion.3), kind=kOutput, calls=%fused_computation.4 | convolution fusion | flops 3223322624 | bytes 3145728 | tf_op jit(solution)/shard_map/dot_general | solution.py:26
  95.3 0.7 fusion.12
  96.1 1.9 %fusion.2 = f32[512,512]{1,0:T(8,128)S(1)} fusion(f32[512,512]{1,0:T(8,128)S(1)} %fusion.12), kind=kOutput, calls=%fused_computation.7 | convolution fusion | flops 1611399168 | bytes 2097152 | tf_op jit(solution)/shard_map/dot_general | solution.py:24
  98.0 2.0 %fusion.13 = f32[512,1024]{1,0:T(8,128)S(1)} fusion(f32[512,512]{1,0:T(8,128)S(1)} %fusion.2, bf16[512,1024]{1,0:T(8,128)(2,1)S(1)} %add_convert_fusion), kind=kOutput, calls=%fused_computation.23 | convolution fusion | flops 3221225472 | bytes 4194304 | tf_op jit(solution)/shard_map/dot_general | solution.py:26
  100.0 0.0 copy-start.2
  100.1 0.4 copy.7
  100.5 0.5 broadcast.39
  101.0 2.3 %reduce.1 = bf16[1024,8]{1,0:T(8,128)(2,1)S(1)} reduce(bf16[1024,1,8]{2,1,0:T(2,128)(2,1)S(1)} %bitcast.37, bf16[]{:T(256)} %broadcast.39), dimensions={1}, to_apply=%bitcast.18.reduce_sub_computation | reduce | bytes 32770
  103.3 0.3 reshape.19
  103.5 11.9 %all_to_all.28 = bf16[8,2,512]{2,1,0:T(2,128)(2,1)S(1)} all-to-all(bf16[8,2,512]{2,1,0:T(2,128)(2,1)S(1)} %reshape.19), channel_id=1, replica_groups=mesh['sx'=4,'sz'=8,'sc'=2,'tensor'=8] {'tensor'}, dimensions={0} | all-to-all | bytes 32768 | tf_op jit(solution)/shard_map/all_to_all | solution.py:51
  115.5 0.7 reshape.20
  116.2 0.7 convert_multiply_fusion.1
  116.9 0.2 copy.8
  117.1 0.0 copy-done.2
  117.1 0.0 copy-start.1
  117.1 0.6 multiply_subtract_fusion
  117.7 0.0 copy-done.1
  (1 shorter events, 0.0 us)
Async XLA Ops:
  7.2 74.4 %all-gather.2.cloned.1.call-start = ((), (), s32[]{:S(2)}) async-start(), calls=%async_computation.2 | async-start | bytes 1572864 | tf_op jit(solution)/shard_map/all_gather | solution.py:38
  86.9 1.9 %copy-start = (bf16[1,512,1024]{2,1,0:T(8,128)(2,1)S(1)}, bf16[1,512,1024]{2,1,0:T(8,128)(2,1)}, u32[]{:S(2)}) copy-start(bf16[1,512,1024]{2,1,0:T(8,128)(2,1)} %all-gather.2.cloned.1.call-done) | copy-start | bytes 3145732
  100.0 17.0 %copy-start.2 = (f32[8,8,128]{2,1,0:T(8,128)S(1)}, f32[8,8,128]{2,1,0:T(8,128)}, u32[]{:S(2)}) copy-start(f32[8,8,128]{2,1,0:T(8,128)} %param.5) | copy-start | bytes 98308
  117.1 0.6 copy-start.1
Sparse Core Ops, SparseCore 0:
  60.6 20.9 all-gather.1

commit v3 on v2

--- a/solution.py
+++ b/solution.py
@@ -33,10 +33,14 @@
     n_tensor = lax.axis_size("tensor")
     new_momentum = mu_decay * momentum + grad
     advance = (grad + mu_decay * new_momentum).astype(jnp.bfloat16)
-    mine = lax.all_to_all(advance, "tensor", split_axis=0, concat_axis=2, tiled=True)
+    n_shard = 1
     for axis in SHARD_AXES:
-        mine = lax.all_gather(mine, axis, axis=1, tiled=True)
-    whole = mine[0]
+        n_shard *= lax.axis_size(axis)
+    sent = jnp.broadcast_to(advance[None], (n_shard,) + advance.shape)
+    sent = sent.reshape(n_shard * mats, rows_local, cols_local)
+    got = lax.all_to_all(sent, SHARD_AXES + ("tensor",), split_axis=0, concat_axis=0, tiled=True)
+    got = got.reshape(n_shard, n_tensor, rows_local, cols_local).transpose(0, 2, 1, 3)
+    whole = got.reshape(n_shard * rows_local, n_tensor * cols_local)
     wide = whole.astype(jnp.float32)
     frob = jnp.sqrt(jnp.sum(wide * wide)) + epsilon
     iterate = (wide / frob).astype(jnp.bfloat16)
@@ -44,7 +48,7 @@
         gram = jnp.dot(iterate, iterate.T, preferred_element_type=jnp.float32)
         iterate = polish(iterate, gram)
     block = 0
-    for axis in reversed(SHARD_AXES):
+    for axis in SHARD_AXES:
         block = block * lax.axis_size(axis) + lax.axis_index(axis)
     start = block * rows_local
     rows = lax.dynamic_slice_in_dim(iterate, start, rows_local, axis=0)

time: 125 us -> 89.1 us (0.71)
  blocking collectives: 63.7 us -> 10.1 us
  starting transfers between devices: 0.04 us -> 22.3 us
  between operations: 14.9 us -> 1.46 us
  waiting for transfers between devices: 21.1 us -> 31.7 us
  matrix products: 15.3 us -> 13.6 us
    all_gather x2 -> x0, blocking collectives: 37.8 us -> none  [on_device(): mine = lax.all_gather(mine, axis, axis=1, tiled=True)]
    all_to_all x0 -> x1, waiting for transfers between devices: none -> 31.7 us  [on_device(): lax.all_to_all(sent, SHARD_AXES + ('tensor',), split_axis=0, concat_axis=...]
    all_to_all x0 -> x1, starting transfers between devices: none -> 22.3 us  [on_device(): lax.all_to_all(sent, SHARD_AXES + ('tensor',), split_axis=0, concat_axis=...]
    all_gather x1 -> x0, waiting for transfers between devices: 21.1 us -> none  [on_device(): mine = lax.all_gather(mine, axis, axis=1, tiled=True)]
    all_to_all x1 -> x0, blocking collectives: 14 us -> none  [on_device(): lax.all_to_all(advance, 'tensor', split_axis=0, concat_axis=2, tiled=True)]
    all_to_all x1, blocking collectives: 11.9 us -> 10.1 us  [on_device(): lax.all_to_all(rows[None], 'tensor', split_axis=2, concat_axis=0, tiled=T...]
    dot_general x3, matrix products: 3.78 us -> 2.22 us  [on_device(): gram = jnp.dot(iterate, iterate.T, preferred_element_type=jnp.float32)]
where the time goes in v3:
time: 89.1 us; the launch traced here: 88.9 us
  waiting for transfers between devices  31.7 us (36%)
  starting transfers between devices  22.3 us (25%)
  matrix products  13.6 us (15%)
  blocking collectives  10.1 us (11%)
  other arithmetic  6.39 us (7%)
  local copies, waits for them, and re-layouts  3.27 us (4%)
  between operations  1.46 us (2%)
    all_to_all x1, waiting for transfers between devices, on_device(): lax.all_to_all(sent, SHARD_AXES + ('tensor',), split_axis=0, concat_axis=...  31.7 us
    all_to_all x1, starting transfers between devices, on_device(): lax.all_to_all(sent, SHARD_AXES + ('tensor',), split_axis=0, concat_axis=...  22.3 us
    all_to_all x1, blocking collectives, on_device(): lax.all_to_all(rows[None], 'tensor', split_axis=2, concat_axis=0, tiled=T...  10.1 us
    dot_general x3, matrix products, polish(): mixed = jnp.dot(poly, wide, precision=lax.Precision.HIGHEST)  5.72 us
    dot_general x3, matrix products, polish(): squared = jnp.dot(gram, gram, precision=lax.Precision.HIGHEST)  5.7 us
    unnamed x1, other arithmetic  2.27 us
    dot_general x3, matrix products, on_device(): gram = jnp.dot(iterate, iterate.T, preferred_element_type=jnp.float32)  2.22 us
  transfers between devices with their start and end apart: 1, of which 1 were waited for; matrix products, arithmetic and copies ran while one was open for 0% of the time, Pallas kernels for 0%

profile of v3, /device:TPU:1, one launch (start us, length us, event | category | flops | bytes accessed | tf_op | source)
XLA Modules:
  0.0 88.9 jit_solution(1411848946740032259)
XLA Ops:
  0.6 1.4 %add_convert_fusion.2 = (bf16[8,8,128]{2,1,0:T(8,128)(2,1)S(1)}, f32[8,8,128]{2,1,0:T(8,128)}) fusion(f32[8,8,128]{2,1,0:T(8,128)} %param.3, f32[8,8,128]{2,1,0:T(8,128)} %param.4), kind=kLoop, calls=%fused_computation.16 | loop fusion | flops 40960 | bytes 114688 | tf_op jit(solution)/shard_map/convert_element_type | solution.py:35
  2.0 1.2 %broadcast_in_dim.4 = bf16[64,8,8,128]{3,2,1,0:T(8,128)(2,1)} broadcast(bf16[8,8,128]{2,1,0:T(8,128)(2,1)S(1)} %get-tuple-element.3), dimensions={1,2,3} | broadcast | bytes 1064960 | tf_op jit(solution)/shard_map/broadcast_in_dim | solution.py:39
  3.3 22.3 %all-to-all-start = ((bf16[512,8,128]{2,1,0:T(8,128)(2,1)}), bf16[512,8,128]{2,1,0:T(8,128)(2,1)S(1)}, u32[]{:S(2)}, u32[]{:S(2)}) async-start(bf16[512,8,128]{2,1,0:T(8,128)(2,1)} %bitcast), calls=%async_computation | async-start | bytes 2097152 | tf_op jit(solution)/shard_map/all_to_all | solution.py:41
  25.6 31.7 %all-to-all-done = bf16[512,8,128]{2,1,0:T(8,128)(2,1)S(1)} async-done(((bf16[512,8,128]{2,1,0:T(8,128)(2,1)}), bf16[512,8,128]{2,1,0:T(8,128)(2,1)S(1)}, u32[]{:S(2)}, u32[]{:S(2)}) %all-to-all-start) | async-done | bytes 1048608 | tf_op jit(solution)/shard_map/all_to_all | solution.py:41
  57.3 1.1 %fusion = f32[]{:T(128)} fusion(bf16[512,8,128]{2,1,0:T(8,128)(2,1)S(1)} %all-to-all-done), kind=kLoop, calls=%fused_computation.2 | loop fusion | flops 1572863 | bytes 1048580 | tf_op jit(solution)/shard_map/reduce_sum | solution.py:45
  59.1 0.2 fusion.1
  59.3 0.7 fusion.7
  60.1 1.9 %fusion.4 = f32[512,512]{1,0:T(8,128)S(1)} fusion(f32[512,512]{1,0:T(8,128)S(1)} %fusion.7), kind=kOutput, calls=%fused_computation.11 | convolution fusion | flops 1611399168 | bytes 2097152 | tf_op jit(solution)/shard_map/dot_general | solution.py:24
  62.0 1.9 %add_convert_fusion.1 = bf16[512,1024]{1,0:T(8,128)(2,1)S(1)} fusion(bf16[512,1024]{1,0:T(8,128)(2,1)S(1)} %bitcast.37, f32[512,512]{1,0:T(8,128)S(1)} %fusion.4), kind=kOutput, calls=%fused_computation.5 | convolution fusion | flops 3223322624 | bytes 3145728 | tf_op jit(solution)/shard_map/dot_general | solution.py:26
  63.9 0.7 fusion.8
  64.6 1.9 %fusion.3 = f32[512,512]{1,0:T(8,128)S(1)} fusion(f32[512,512]{1,0:T(8,128)S(1)} %fusion.8), kind=kOutput, calls=%fused_computation.9 | convolution fusion | flops 1611399168 | bytes 2097152 | tf_op jit(solution)/shard_map/dot_general | solution.py:24
  66.5 1.8 %add_convert_fusion = bf16[512,1024]{1,0:T(8,128)(2,1)S(1)} fusion(bf16[512,1024]{1,0:T(8,128)(2,1)S(1)} %add_convert_fusion.1, f32[512,512]{1,0:T(8,128)S(1)} %fusion.3), kind=kOutput, calls=%fused_computation.4 | convolution fusion | flops 3223322624 | bytes 3145728 | tf_op jit(solution)/shard_map/dot_general | solution.py:26
  68.4 0.7 fusion.9
  69.1 1.9 %fusion.2 = f32[512,512]{1,0:T(8,128)S(1)} fusion(f32[512,512]{1,0:T(8,128)S(1)} %fusion.9), kind=kOutput, calls=%fused_computation.7 | convolution fusion | flops 1611399168 | bytes 2097152 | tf_op jit(solution)/shard_map/dot_general | solution.py:24
  71.0 2.0 %fusion.10 = f32[512,1024]{1,0:T(8,128)S(1)} fusion(f32[512,512]{1,0:T(8,128)S(1)} %fusion.2, bf16[512,1024]{1,0:T(8,128)(2,1)S(1)} %add_convert_fusion), kind=kOutput, calls=%fused_computation.22 | convolution fusion | flops 3221225472 | bytes 4194304 | tf_op jit(solution)/shard_map/dot_general | solution.py:26
  73.0 0.0 copy-start.1
  73.1 0.4 copy.7
  73.5 0.5 broadcast.48
  74.0 2.3 %reduce.3 = bf16[1024,8]{1,0:T(8,128)(2,1)S(1)} reduce(bf16[1024,1,8]{2,1,0:T(2,128)(2,1)S(1)} %bitcast.34, bf16[]{:T(256)} %broadcast.48), dimensions={1}, to_apply=%bitcast.12.reduce_sub_computation | reduce | bytes 32770
  76.3 0.3 reshape.34
  76.5 10.1 %all_to_all.14 = bf16[8,2,512]{2,1,0:T(2,128)(2,1)S(1)} all-to-all(bf16[8,2,512]{2,1,0:T(2,128)(2,1)S(1)} %reshape.34), channel_id=1, replica_groups=mesh['sx'=4,'sz'=8,'sc'=2,'tensor'=8] {'tensor'}, dimensions={0} | all-to-all | bytes 32768 | tf_op jit(solution)/shard_map/all_to_all | solution.py:55
  86.6 0.7 reshape.35
  87.3 0.7 convert_multiply_fusion.1
  88.1 0.2 copy.8
  88.2 0.0 copy-done.1
  88.2 0.0 copy-start
  88.2 0.6 multiply_subtract_fusion
  88.9 0.0 copy-done
  (1 shorter events, 0.0 us)
Async XLA Ops:
  3.3 54.0 %all-to-all-start = ((bf16[512,8,128]{2,1,0:T(8,128)(2,1)}), bf16[512,8,128]{2,1,0:T(8,128)(2,1)S(1)}, u32[]{:S(2)}, u32[]{:S(2)}) async-start(bf16[512,8,128]{2,1,0:T(8,128)(2,1)} %bitcast), calls=%async_computation | async-start | bytes 2097152 | tf_op jit(solution)/shard_map/all_to_all | solution.py:41
  73.0 15.2 %copy-start.1 = (f32[8,8,128]{2,1,0:T(8,128)S(1)}, f32[8,8,128]{2,1,0:T(8,128)}, u32[]{:S(2)}) copy-start(f32[8,8,128]{2,1,0:T(8,128)} %param.5) | copy-start | bytes 98308
  88.2 0.6 copy-start

commit v4 on v3

--- a/solution.py
+++ b/solution.py
@@ -19,12 +19,19 @@
 epsilon = 1e-07
 
 
-def polish(iterate, gram):
-    wide = iterate.astype(jnp.float32)
-    squared = jnp.dot(gram, gram, precision=lax.Precision.HIGHEST)
-    poly = second_coef * gram + third_coef * squared
-    mixed = jnp.dot(poly, wide, precision=lax.Precision.HIGHEST)
-    fresh = first_coef * wide + mixed
+def split_dot(wide_lhs, rhs):
+    high = wide_lhs.astype(jnp.bfloat16)
+    low = (wide_lhs - high.astype(jnp.float32)).astype(jnp.bfloat16)
+    both = jnp.concatenate([high, low], axis=1)
+    return jnp.dot(both, jnp.concatenate([rhs, rhs], axis=0), preferred_element_type=jnp.float32)
+
+
+def polish(iterate, gram, rows=None):
+    squared_rows = gram if rows is None else rows(gram)
+    squared = jnp.dot(squared_rows, gram, precision=lax.Precision.HIGH)
+    poly = second_coef * squared_rows + third_coef * squared
+    head = iterate if rows is None else rows(iterate)
+    fresh = first_coef * head.astype(jnp.float32) + split_dot(poly, iterate)
     return fresh.astype(jnp.bfloat16)
 
 
@@ -44,15 +51,19 @@
     wide = whole.astype(jnp.float32)
     frob = jnp.sqrt(jnp.sum(wide * wide)) + epsilon
     iterate = (wide / frob).astype(jnp.bfloat16)
-    for step in range(ITERS):
-        gram = jnp.dot(iterate, iterate.T, preferred_element_type=jnp.float32)
-        iterate = polish(iterate, gram)
     block = 0
     for axis in SHARD_AXES:
         block = block * lax.axis_size(axis) + lax.axis_index(axis)
     start = block * rows_local
-    rows = lax.dynamic_slice_in_dim(iterate, start, rows_local, axis=0)
-    ortho = lax.all_to_all(rows[None], "tensor", split_axis=2, concat_axis=0, tiled=True)
+
+    def mine(full):
+        return lax.dynamic_slice_in_dim(full, start, rows_local, axis=0)
+
+    for step in range(ITERS):
+        gram = jnp.dot(iterate, iterate.T, preferred_element_type=jnp.float32)
+        iterate = polish(iterate, gram, mine if step == ITERS - 1 else None)
+    pieces = iterate.reshape(rows_local, n_tensor, cols_local).transpose(1, 0, 2)
+    ortho = lax.all_to_all(pieces, "tensor", split_axis=0, concat_axis=0, tiled=True)
     width = cols_local * n_tensor
     update = update_gain * math.sqrt(width) * ortho.astype(jnp.float32)
     new_weight = weight - learn_rate * (update + weight_decay * weight)

time: 89.1 us -> 78.2 us (0.88)
  matrix products: 13.6 us -> 7.77 us
  other arithmetic: 6.39 us -> 3.38 us
  local copies, waits for them, and re-layouts: 3.27 us -> 1.23 us
    dot_general x6, matrix products: 11.4 us -> 5.54 us  [the longest x3 2.93 us: split_dot(): jnp.dot(both, jnp.concatenate([rhs, rhs], axis=0), preferred_element_type...]
    unnamed x1 -> x0, other arithmetic: 2.27 us -> none
    unnamed x7 -> x2, local copies, waits for them, and re-layouts: 1.48 us -> 0.01 us
where the time goes in v4:
time: 78.2 us; the launch traced here: 77.9 us
  waiting for transfers between devices  31.9 us (41%)
  starting transfers between devices  22.1 us (28%)
  blocking collectives  10.1 us (13%)
  matrix products  7.77 us (10%)
  other arithmetic  3.38 us (4%)
  between operations  1.4 us (2%)
  local copies, waits for them, and re-layouts  1.23 us (2%)
    all_to_all x1, waiting for transfers between devices, on_device(): lax.all_to_all(sent, SHARD_AXES + ('tensor',), split_axis=0, concat_axis=...  31.9 us
    all_to_all x1, starting transfers between devices, on_device(): lax.all_to_all(sent, SHARD_AXES + ('tensor',), split_axis=0, concat_axis=...  22.1 us
    all_to_all x1, blocking collectives, on_device(): lax.all_to_all(pieces, 'tensor', split_axis=0, concat_axis=0, tiled=True)  10.1 us
    dot_general x3, matrix products, split_dot(): jnp.dot(both, jnp.concatenate([rhs, rhs], axis=0), preferred_element_type...  2.93 us
    dot_general x3, matrix products, polish(): squared = jnp.dot(squared_rows, gram, precision=lax.Precision.HIGH)  2.61 us
    dot_general x3, matrix products, on_device(): gram = jnp.dot(iterate, iterate.T, preferred_element_type=jnp.float32)  2.23 us
  transfers between devices with their start and end apart: 1, of which 1 were waited for; matrix products, arithmetic and copies ran while one was open for 0% of the time, Pallas kernels for 0%

profile of v4, /device:TPU:1, one launch (start us, length us, event | category | flops | bytes accessed | tf_op | source)
XLA Modules:
  0.0 77.9 jit_solution(15527119829115122865)
XLA Ops:
  0.6 1.4 %add_convert_fusion.2 = (bf16[8,8,128]{2,1,0:T(8,128)(2,1)S(1)}, f32[8,8,128]{2,1,0:T(8,128)}) fusion(f32[8,8,128]{2,1,0:T(8,128)} %param.3, f32[8,8,128]{2,1,0:T(8,128)} %param.4), kind=kLoop, calls=%fused_computation.37 | loop fusion | flops 40960 | bytes 114688 | tf_op jit(solution)/shard_map/convert_element_type | solution.py:42
  2.0 1.2 %broadcast_in_dim.2 = bf16[64,8,8,128]{3,2,1,0:T(8,128)(2,1)} broadcast(bf16[8,8,128]{2,1,0:T(8,128)(2,1)S(1)} %get-tuple-element.11), dimensions={1,2,3} | broadcast | bytes 1064960 | tf_op jit(solution)/shard_map/broadcast_in_dim | solution.py:46
  3.3 22.1 %all-to-all-start = ((bf16[512,8,128]{2,1,0:T(8,128)(2,1)}), bf16[512,8,128]{2,1,0:T(8,128)(2,1)S(1)}, u32[]{:S(2)}, u32[]{:S(2)}) async-start(bf16[512,8,128]{2,1,0:T(8,128)(2,1)} %bitcast), calls=%async_computation | async-start | bytes 2097152 | tf_op jit(solution)/shard_map/all_to_all | solution.py:48
  25.4 31.9 %all-to-all-done = bf16[512,8,128]{2,1,0:T(8,128)(2,1)S(1)} async-done(((bf16[512,8,128]{2,1,0:T(8,128)(2,1)}), bf16[512,8,128]{2,1,0:T(8,128)(2,1)S(1)}, u32[]{:S(2)}, u32[]{:S(2)}) %all-to-all-start) | async-done | bytes 1048608 | tf_op jit(solution)/shard_map/all_to_all | solution.py:48
  57.3 1.1 %fusion = f32[]{:T(128)} fusion(bf16[512,8,128]{2,1,0:T(8,128)(2,1)S(1)} %all-to-all-done), kind=kLoop, calls=%fused_computation.2 | loop fusion | flops 1572863 | bytes 1048580 | tf_op jit(solution)/shard_map/reduce_sum | solution.py:52
  59.1 0.2 fusion.1
  59.3 0.7 fusion.44
  60.1 1.1 %subtract_convert_fusion.1 = (bf16[512,512]{0,1:T(8,128)(2,1)S(1)}, bf16[512,512]{0,1:T(8,128)(2,1)S(1)}) fusion(f32[512,512]{0,1:T(8,128)S(1)} %fusion.44), kind=kOutput, calls=%fused_computation.34 | convolution fusion | flops 807141376 | bytes 2097152 | tf_op jit(solution)/shard_map/dot_general | solution.py:31
  61.2 1.3 %add_convert_fusion.1 = bf16[512,1024]{1,0:T(8,128)(2,1)S(1)} fusion(bf16[512,1024]{1,0:T(8,128)(2,1)S(1)} %bitcast.22, bf16[512,512]{0,1:T(8,128)(2,1)S(1)} %get-tuple-element.9, bf16[512,512]{0,1:T(8,128)(2,1)S(1)} %get-tuple-element.10), kind=kOutput, calls=%fused_computation.17 | convolution fusion | flops 1082130432 | bytes 3145728 | tf_op jit(solution)/shard_map/dot_general | solution.py:26
  62.5 0.7 fusion.45
  63.2 1.1 %subtract_convert_fusion = (bf16[512,512]{0,1:T(8,128)(2,1)S(1)}, bf16[512,512]{0,1:T(8,128)(2,1)S(1)}) fusion(f32[512,512]{0,1:T(8,128)S(1)} %fusion.45), kind=kOutput, calls=%fused_computation.33 | convolution fusion | flops 807141376 | bytes 2097152 | tf_op jit(solution)/shard_map/dot_general | solution.py:31
  64.4 1.3 %add_convert_fusion = bf16[512,1024]{1,0:T(8,128)(2,1)S(1)} fusion(bf16[512,1024]{1,0:T(8,128)(2,1)S(1)} %add_convert_fusion.1, bf16[512,512]{0,1:T(8,128)(2,1)S(1)} %get-tuple-element.7, bf16[512,512]{0,1:T(8,128)(2,1)S(1)} %get-tuple-element.8), kind=kOutput, calls=%fused_computation.16 | convolution fusion | flops 1082130432 | bytes 3145728 | tf_op jit(solution)/shard_map/dot_general | solution.py:26
  65.6 0.7 fusion.46
  66.4 0.4 subtract_convert_fusion.2
  66.8 0.0 copy-start
  66.8 0.4 fusion.26
  67.1 10.1 %all_to_all.10 = bf16[8,8,128]{2,1,0:T(8,128)(2,1)S(1)} all-to-all(bf16[8,8,128]{2,1,0:T(8,128)(2,1)S(1)} %fusion.26), channel_id=1, replica_groups=mesh['sx'=4,'sz'=8,'sc'=2,'tensor'=8] {'tensor'}, dimensions={0} | all-to-all | bytes 32768 | tf_op jit(solution)/shard_map/all_to_all | solution.py:66
  77.2 0.0 copy-done
  77.2 0.6 multiply_subtract_fusion
Async XLA Ops:
  3.3 54.0 %all-to-all-start = ((bf16[512,8,128]{2,1,0:T(8,128)(2,1)}), bf16[512,8,128]{2,1,0:T(8,128)(2,1)S(1)}, u32[]{:S(2)}, u32[]{:S(2)}) async-start(bf16[512,8,128]{2,1,0:T(8,128)(2,1)} %bitcast), calls=%async_computation | async-start | bytes 2097152 | tf_op jit(solution)/shard_map/all_to_all | solution.py:48
  66.8 10.5 %copy-start = (f32[8,8,128]{2,1,0:T(8,128)S(1)}, f32[8,8,128]{2,1,0:T(8,128)}, u32[]{:S(2)}) copy-start(f32[8,8,128]{2,1,0:T(8,128)} %param.5) | copy-start | bytes 98308

commit v5 on v4

--- a/solution.py
+++ b/solution.py
@@ -3,7 +3,10 @@
 import jax
 import jax.numpy as jnp
 from jax import lax
+from jax.experimental import pallas as pl
+from jax.experimental.pallas import tpu as pltpu
 from jax.sharding import PartitionSpec as P
+import functools
 
 ITERS = 3
 SHARD_AXES = ("sx", "sz", "sc")
@@ -19,6 +22,119 @@
 epsilon = 1e-07
 
 
+MESH = pl.DeviceIdType.MESH
+
+
+def shard_coords(index, sizes):
+    coords = []
+    for size in reversed(sizes):
+        coords.append(index % size)
+        index = index // size
+    return tuple(reversed(coords))
+
+
+def gather_kernel(sizes, n_tensor, adv_ref, out_ref, row_buf, whole_buf,
+                  send1, recv1, send2, recv2, local_sem):
+    mats, rows, cols = adv_ref.shape
+    n_shard = 1
+    for size in sizes:
+        n_shard *= size
+    here = tuple(lax.axis_index(a) for a in SHARD_AXES)
+    t = lax.axis_index("tensor")
+    me = 0
+    for axis, size in zip(SHARD_AXES, sizes):
+        me = me * size + lax.axis_index(axis)
+
+    def shard_peer(k):
+        return shard_coords(lax.rem(me + k, n_shard), sizes)
+
+    barrier = pltpu.get_barrier_semaphore()
+    for k in range(1, n_tensor):
+        pl.semaphore_signal(barrier, inc=1, device_id=here + (lax.rem(t + k, n_tensor),),
+                            device_id_type=MESH)
+
+    def greet(k, carry):
+        pl.semaphore_signal(barrier, inc=1, device_id=shard_peer(k) + (t,), device_id_type=MESH)
+        return carry
+
+    lax.fori_loop(1, n_shard, greet, 0)
+    pl.semaphore_wait(barrier, n_tensor - 1 + n_shard - 1)
+
+    my_cols = pl.ds(pl.multiple_of(t * cols, cols), cols)
+    own = pltpu.make_async_copy(adv_ref.at[t], row_buf.at[:, my_cols], local_sem)
+    own.start()
+    firsts = []
+    for k in range(1, n_tensor):
+        peer = lax.rem(t + k, n_tensor)
+        copy = pltpu.make_async_remote_copy(
+            src_ref=adv_ref.at[peer], dst_ref=row_buf.at[:, my_cols],
+            send_sem=send1.at[peer], recv_sem=recv1.at[t],
+            device_id=here + (peer,), device_id_type=MESH)
+        copy.start()
+        firsts.append(copy)
+    own.wait()
+    for k in range(1, n_tensor):
+        peer = lax.rem(t + k, n_tensor)
+        peer_cols = pl.ds(pl.multiple_of(peer * cols, cols), cols)
+        pltpu.make_async_remote_copy(
+            src_ref=adv_ref.at[t], dst_ref=row_buf.at[:, peer_cols],
+            send_sem=send1.at[peer], recv_sem=recv1.at[peer],
+            device_id=here + (peer,), device_id_type=MESH).wait_recv()
+        firsts[k - 1].wait_send()
+
+    my_rows = pl.ds(pl.multiple_of(me * rows, rows), rows)
+    own = pltpu.make_async_copy(row_buf, whole_buf.at[my_rows], local_sem)
+    own.start()
+
+    def send(k, carry):
+        peer = lax.rem(me + k, n_shard)
+        pltpu.make_async_remote_copy(
+            src_ref=row_buf, dst_ref=whole_buf.at[my_rows],
+            send_sem=send2.at[peer], recv_sem=recv2.at[me],
+            device_id=shard_coords(peer, sizes) + (t,), device_id_type=MESH).start()
+        return carry
+
+    lax.fori_loop(1, n_shard, send, 0)
+    own.wait()
+
+    def finish(k, carry):
+        peer = lax.rem(me + k, n_shard)
+        peer_rows = pl.ds(pl.multiple_of(peer * rows, rows), rows)
+        copy = pltpu.make_async_remote_copy(
+            src_ref=row_buf, dst_ref=whole_buf.at[peer_rows],
+            send_sem=send2.at[peer], recv_sem=recv2.at[peer],
+            device_id=shard_coords(peer, sizes) + (t,), device_id_type=MESH)
+        copy.wait_recv()
+        copy.wait_send()
+        return carry
+
+    lax.fori_loop(1, n_shard, finish, 0)
+    out_ref[...] = whole_buf[...]
+
+
+def gather(advance, sizes, n_tensor):
+    mats, rows, cols = advance.shape
+    n_shard = 1
+    for size in sizes:
+        n_shard *= size
+    return pl.pallas_call(
+        functools.partial(gather_kernel, sizes, n_tensor),
+        out_shape=jax.ShapeDtypeStruct((n_shard * rows, n_tensor * cols), advance.dtype),
+        in_specs=[pl.BlockSpec(memory_space=pltpu.VMEM)],
+        out_specs=pl.BlockSpec(memory_space=pltpu.VMEM),
+        scratch_shapes=[
+            pltpu.VMEM((rows, n_tensor * cols), advance.dtype),
+            pltpu.VMEM((n_shard * rows, n_tensor * cols), advance.dtype),
+            pltpu.SemaphoreType.DMA((n_tensor,)),
+            pltpu.SemaphoreType.DMA((n_tensor,)),
+            pltpu.SemaphoreType.DMA((n_shard,)),
+            pltpu.SemaphoreType.DMA((n_shard,)),
+            pltpu.SemaphoreType.DMA,
+        ],
+        compiler_params=pltpu.CompilerParams(collective_id=0, has_side_effects=True),
+    )(advance)
+
+
 def split_dot(wide_lhs, rhs):
     high = wide_lhs.astype(jnp.bfloat16)
     low = (wide_lhs - high.astype(jnp.float32)).astype(jnp.bfloat16)
@@ -40,14 +156,8 @@
     n_tensor = lax.axis_size("tensor")
     new_momentum = mu_decay * momentum + grad
     advance = (grad + mu_decay * new_momentum).astype(jnp.bfloat16)
-    n_shard = 1
-    for axis in SHARD_AXES:
-        n_shard *= lax.axis_size(axis)
-    sent = jnp.broadcast_to(advance[None], (n_shard,) + advance.shape)
-    sent = sent.reshape(n_shard * mats, rows_local, cols_local)
-    got = lax.all_to_all(sent, SHARD_AXES + ("tensor",), split_axis=0, concat_axis=0, tiled=True)
-    got = got.reshape(n_shard, n_tensor, rows_local, cols_local).transpose(0, 2, 1, 3)
-    whole = got.reshape(n_shard * rows_local, n_tensor * cols_local)
+    sizes = tuple(lax.axis_size(axis) for axis in SHARD_AXES)
+    whole = gather(advance, sizes, n_tensor)
     wide = whole.astype(jnp.float32)
     frob = jnp.sqrt(jnp.sum(wide * wide)) + epsilon
     iterate = (wide / frob).astype(jnp.bfloat16)

time: 78.2 us -> 73.2 us (0.936)
  Pallas kernels: 0 us -> 50 us
  waiting for transfers between devices: 31.9 us -> 0 us
  starting transfers between devices: 22.1 us -> 0 us
  other arithmetic: 3.38 us -> 4.69 us
  local copies, waits for them, and re-layouts: 1.23 us -> 0.01 us
  blocking collectives: 10.1 us -> 8.98 us
    pallas_call x0 -> x1, Pallas kernels: none -> 50 us  [gather(): pl.pallas_call(functools.partial(gather_kernel, sizes, n_tensor), out_sha...]
    all_to_all x1 -> x0, waiting for transfers between devices: 31.9 us -> none  [on_device(): lax.all_to_all(sent, SHARD_AXES + ('tensor',), split_axis=0, concat_axis=...]
    all_to_all x1 -> x0, starting transfers between devices: 22.1 us -> none  [on_device(): lax.all_to_all(sent, SHARD_AXES + ('tensor',), split_axis=0, concat_axis=...]
    reduce_sum x1, other arithmetic: 1.14 us -> 2.46 us  [on_device(): frob = jnp.sqrt(jnp.sum(wide * wide)) + epsilon]
    broadcast_in_dim x1 -> x0, local copies, waits for them, and re-layouts: 1.23 us -> none  [on_device(): sent = jnp.broadcast_to(advance[None], (n_shard,) + advance.shape)]
    all_to_all x1, blocking collectives: 10.1 us -> 8.98 us  [on_device(): lax.all_to_all(pieces, 'tensor', split_axis=0, concat_axis=0, tiled=True)]
  transfers between devices with their start and end apart: 1 -> 0, of which waited for: 1 -> 0; matrix products, arithmetic and copies ran while one was open for 0% -> 0% of each run, Pallas kernels for 0% -> 0%
where the time goes in v5:
time: 73.2 us; the launch traced here: 72.8 us
  Pallas kernels  50 us (68%)
  blocking collectives  8.98 us (12%)
  matrix products  7.77 us (11%)
  other arithmetic  4.69 us (6%)
  between operations  1.42 us (2%)
    pallas_call x1, Pallas kernels, gather(): pl.pallas_call(functools.partial(gather_kernel, sizes, n_tensor), out_sha...  50 us
    all_to_all x1, blocking collectives, on_device(): lax.all_to_all(pieces, 'tensor', split_axis=0, concat_axis=0, tiled=True)  8.98 us
    dot_general x3, matrix products, split_dot(): jnp.dot(both, jnp.concatenate([rhs, rhs], axis=0), preferred_element_type...  2.93 us
    dot_general x3, matrix products, polish(): squared = jnp.dot(squared_rows, gram, precision=lax.Precision.HIGH)  2.61 us
    reduce_sum x1, other arithmetic, on_device(): frob = jnp.sqrt(jnp.sum(wide * wide)) + epsilon  2.46 us
    dot_general x3, matrix products, on_device(): gram = jnp.dot(iterate, iterate.T, preferred_element_type=jnp.float32)  2.23 us

profile of v5, /device:TPU:1, one launch (start us, length us, event | category | flops | bytes accessed | tf_op | source)
XLA Modules:
  0.0 72.8 jit_solution(9568536411948827034)
XLA Ops:
  0.6 1.4 %add_convert_fusion.2 = (bf16[8,8,128]{2,1,0:T(8,128)(2,1)}, f32[8,8,128]{2,1,0:T(8,128)}) fusion(f32[8,8,128]{2,1,0:T(8,128)} %param.3, f32[8,8,128]{2,1,0:T(8,128)} %param.4), kind=kLoop, calls=%fused_computation.37 | loop fusion | flops 40960 | bytes 114688 | tf_op jit(solution)/shard_map/convert_element_type | solution.py:158
  2.0 50.0 %shard_map.58 = bf16[512,1024]{1,0:T(8,128)(2,1)} custom-call(bf16[8,8,128]{2,1,0:T(8,128)(2,1)} %get-tuple-element.11.adv_ref), custom_call_target="tpu_custom_call" | custom-call | tf_op jit(solution)/shard_map/pallas_call | solution.py:120
  52.0 0.0 copy-start
  52.0 2.5 %fusion = f32[]{:T(128)} fusion(bf16[512,1024]{1,0:T(8,128)(2,1)} %shard_map.58), kind=kLoop, calls=%fused_computation.2 | loop fusion | flops 1572863 | bytes 1048580 | tf_op jit(solution)/shard_map/reduce_sum | solution.py:162
  55.2 0.0 copy-done
  55.2 0.2 fusion.1
  55.4 0.7 %fusion.44 = f32[512,512]{0,1:T(8,128)S(1)} fusion(bf16[512,1024]{1,0:T(8,128)(2,1)S(1)} %fusion.1), kind=kOutput, calls=%fused_computation.48 | convolution fusion | flops 536870912 | bytes 2097152 | tf_op jit(solution)/shard_map/dot_general | solution.py:173
  56.1 1.1 %subtract_convert_fusion.1 = (bf16[512,512]{0,1:T(8,128)(2,1)S(1)}, bf16[512,512]{0,1:T(8,128)(2,1)S(1)}) fusion(f32[512,512]{0,1:T(8,128)S(1)} %fusion.44), kind=kOutput, calls=%fused_computation.34 | convolution fusion | flops 807141376 | bytes 2097152 | tf_op jit(solution)/shard_map/dot_general | solution.py:147
  57.3 1.3 %add_convert_fusion.1 = bf16[512,1024]{1,0:T(8,128)(2,1)S(1)} fusion(bf16[512,1024]{1,0:T(8,128)(2,1)S(1)} %fusion.1, bf16[512,512]{0,1:T(8,128)(2,1)S(1)} %get-tuple-element.9, bf16[512,512]{0,1:T(8,128)(2,1)S(1)} %get-tuple-element.10), kind=kOutput, calls=%fused_computation.17 | convolution fusion | flops 1082130432 | bytes 3145728 | tf_op jit(solution)/shard_map/dot_general | solution.py:142
  58.5 0.7 %fusion.45 = f32[512,512]{0,1:T(8,128)S(1)} fusion(bf16[512,1024]{1,0:T(8,128)(2,1)S(1)} %add_convert_fusion.1), kind=kOutput, calls=%fused_computation.49 | convolution fusion | flops 536870912 | bytes 2097152 | tf_op jit(solution)/shard_map/dot_general | solution.py:173
  59.3 1.1 %subtract_convert_fusion = (bf16[512,512]{0,1:T(8,128)(2,1)S(1)}, bf16[512,512]{0,1:T(8,128)(2,1)S(1)}) fusion(f32[512,512]{0,1:T(8,128)S(1)} %fusion.45), kind=kOutput, calls=%fused_computation.33 | convolution fusion | flops 807141376 | bytes 2097152 | tf_op jit(solution)/shard_map/dot_general | solution.py:147
  60.4 1.3 %add_convert_fusion = bf16[512,1024]{1,0:T(8,128)(2,1)S(1)} fusion(bf16[512,1024]{1,0:T(8,128)(2,1)S(1)} %add_convert_fusion.1, bf16[512,512]{0,1:T(8,128)(2,1)S(1)} %get-tuple-element.7, bf16[512,512]{0,1:T(8,128)(2,1)S(1)} %get-tuple-element.8), kind=kOutput, calls=%fused_computation.16 | convolution fusion | flops 1082130432 | bytes 3145728 | tf_op jit(solution)/shard_map/dot_general | solution.py:142
  61.7 0.7 %fusion.46 = f32[512,512]{1,0:T(8,128)S(1)} fusion(bf16[512,1024]{1,0:T(8,128)(2,1)S(1)} %add_convert_fusion), kind=kOutput, calls=%fused_computation.50 | convolution fusion | flops 536870912 | bytes 2097152 | tf_op jit(solution)/shard_map/dot_general | solution.py:173
  62.5 0.4 subtract_convert_fusion.2
  62.8 0.0 copy-start.1
  62.8 0.4 fusion.26
  63.2 9.0 %all_to_all.5 = bf16[8,8,128]{2,1,0:T(8,128)(2,1)S(1)} all-to-all(bf16[8,8,128]{2,1,0:T(8,128)(2,1)S(1)} %fusion.26), channel_id=1, replica_groups=mesh['sx'=4,'sz'=8,'sc'=2,'tensor'=8] {'tensor'}, dimensions={0} | all-to-all | bytes 32768 | tf_op jit(solution)/shard_map/all_to_all | solution.py:176
  72.2 0.0 copy-done.1
  72.2 0.6 multiply_subtract_fusion
Async XLA Ops:
  52.0 3.2 %copy-start = (bf16[512,1024]{1,0:T(8,128)(2,1)S(1)}, bf16[512,1024]{1,0:T(8,128)(2,1)}, u32[]{:S(2)}) copy-start(bf16[512,1024]{1,0:T(8,128)(2,1)} %shard_map.58) | copy-start | bytes 3145732
  62.8 9.4 %copy-start.1 = (f32[8,8,128]{2,1,0:T(8,128)S(1)}, f32[8,8,128]{2,1,0:T(8,128)}, u32[]{:S(2)}) copy-start(f32[8,8,128]{2,1,0:T(8,128)} %param.5) | copy-start | bytes 98308

commit v6 on v5

--- a/solution.py
+++ b/solution.py
@@ -135,6 +135,148 @@
     )(advance)
 
 
+def gather2_kernel(sizes, n_tensor, adv_ref, out_ref, row_buf, whole_buf,
+                   send1, recv1, send2, recv2, fwd, local_sem):
+    mats, rows, cols = adv_ref.shape
+    n_core = sizes[-1]
+    n_chip = 1
+    for size in sizes[:-1]:
+        n_chip *= size
+    n_shard = n_chip * n_core
+    here = tuple(lax.axis_index(a) for a in SHARD_AXES)
+    t = lax.axis_index("tensor")
+    me = 0
+    for axis, size in zip(SHARD_AXES, sizes):
+        me = me * size + lax.axis_index(axis)
+    core = lax.rem(me, n_core)
+    chip = me // n_core
+
+    def device(index):
+        return shard_coords(index, sizes) + (t,)
+
+    def chip_peer(k):
+        return lax.rem(chip + k, n_chip) * n_core + core
+
+    def sibling(j):
+        return chip * n_core + lax.rem(core + j, n_core)
+
+    barrier = pltpu.get_barrier_semaphore()
+    for k in range(1, n_tensor):
+        pl.semaphore_signal(barrier, inc=1, device_id=here + (lax.rem(t + k, n_tensor),),
+                            device_id_type=MESH)
+
+    def greet(k, carry):
+        pl.semaphore_signal(barrier, inc=1, device_id=device(chip_peer(k)), device_id_type=MESH)
+        return carry
+
+    lax.fori_loop(1, n_chip, greet, 0)
+    for j in range(1, n_core):
+        pl.semaphore_signal(barrier, inc=1, device_id=device(sibling(j)), device_id_type=MESH)
+    pl.semaphore_wait(barrier, n_tensor - 1 + n_chip - 1 + n_core - 1)
+
+    my_cols = pl.ds(pl.multiple_of(t * cols, cols), cols)
+    own = pltpu.make_async_copy(adv_ref.at[t], row_buf.at[:, my_cols], local_sem)
+    own.start()
+    firsts = []
+    for k in range(1, n_tensor):
+        peer = lax.rem(t + k, n_tensor)
+        copy = pltpu.make_async_remote_copy(
+            src_ref=adv_ref.at[peer], dst_ref=row_buf.at[:, my_cols],
+            send_sem=send1.at[peer], recv_sem=recv1.at[t],
+            device_id=here + (peer,), device_id_type=MESH)
+        copy.start()
+        firsts.append(copy)
+    own.wait()
+    for k in range(1, n_tensor):
+        peer = lax.rem(t + k, n_tensor)
+        peer_cols = pl.ds(pl.multiple_of(peer * cols, cols), cols)
+        pltpu.make_async_remote_copy(
+            src_ref=adv_ref.at[t], dst_ref=row_buf.at[:, peer_cols],
+            send_sem=send1.at[peer], recv_sem=recv1.at[peer],
+            device_id=here + (peer,), device_id_type=MESH).wait_recv()
+        firsts[k - 1].wait_send()
+
+    def rows_of(index):
+        return pl.ds(pl.multiple_of(index * rows, rows), rows)
+
+    def direct(dest):
+        return pltpu.make_async_remote_copy(
+            src_ref=row_buf, dst_ref=whole_buf.at[rows_of(me)],
+            send_sem=send2.at[dest], recv_sem=recv2.at[me],
+            device_id=device(dest), device_id_type=MESH)
+
+    def send(k, carry):
+        direct(chip_peer(k)).start()
+        return carry
+
+    lax.fori_loop(1, n_chip, send, 0)
+    for j in range(1, n_core):
+        direct(sibling(j)).start()
+    own = pltpu.make_async_copy(row_buf, whole_buf.at[rows_of(me)], local_sem)
+    own.start()
+
+    def forward(source, dest):
+        return pltpu.make_async_remote_copy(
+            src_ref=whole_buf.at[rows_of(source)], dst_ref=whole_buf.at[rows_of(source)],
+            send_sem=fwd.at[source], recv_sem=recv2.at[source],
+            device_id=device(dest), device_id_type=MESH)
+
+    def relay(k, carry):
+        source = chip_peer(k)
+        pltpu.make_async_remote_copy(
+            src_ref=row_buf, dst_ref=whole_buf.at[rows_of(source)],
+            send_sem=send2.at[source], recv_sem=recv2.at[source],
+            device_id=device(source), device_id_type=MESH).wait_recv()
+        for j in range(1, n_core):
+            forward(source, sibling(j)).start()
+        return carry
+
+    lax.fori_loop(1, n_chip, relay, 0)
+    own.wait()
+
+    def settle(k, carry):
+        source = chip_peer(k)
+        direct(source).wait_send()
+        for j in range(1, n_core):
+            forward(source, sibling(j)).wait_send()
+            other = source - core + lax.rem(core + j, n_core)
+            forward(other, sibling(j)).wait_recv()
+        return carry
+
+    lax.fori_loop(1, n_chip, settle, 0)
+    for j in range(1, n_core):
+        direct(sibling(j)).wait_send()
+        pltpu.make_async_remote_copy(
+            src_ref=row_buf, dst_ref=whole_buf.at[rows_of(sibling(j))],
+            send_sem=send2.at[sibling(j)], recv_sem=recv2.at[sibling(j)],
+            device_id=device(sibling(j)), device_id_type=MESH).wait_recv()
+    out_ref[...] = whole_buf[...]
+
+
+def gather2(advance, sizes, n_tensor):
+    mats, rows, cols = advance.shape
+    n_shard = 1
+    for size in sizes:
+        n_shard *= size
+    return pl.pallas_call(
+        functools.partial(gather2_kernel, sizes, n_tensor),
+        out_shape=jax.ShapeDtypeStruct((n_shard * rows, n_tensor * cols), advance.dtype),
+        in_specs=[pl.BlockSpec(memory_space=pltpu.VMEM)],
+        out_specs=pl.BlockSpec(memory_space=pltpu.VMEM),
+        scratch_shapes=[
+            pltpu.VMEM((rows, n_tensor * cols), advance.dtype),
+            pltpu.VMEM((n_shard * rows, n_tensor * cols), advance.dtype),
+            pltpu.SemaphoreType.DMA((n_tensor,)),
+            pltpu.SemaphoreType.DMA((n_tensor,)),
+            pltpu.SemaphoreType.DMA((n_shard,)),
+            pltpu.SemaphoreType.DMA((n_shard,)),
+            pltpu.SemaphoreType.DMA((n_shard,)),
+            pltpu.SemaphoreType.DMA,
+        ],
+        compiler_params=pltpu.CompilerParams(collective_id=0, has_side_effects=True),
+    )(advance)
+
+
 def split_dot(wide_lhs, rhs):
     high = wide_lhs.astype(jnp.bfloat16)
     low = (wide_lhs - high.astype(jnp.float32)).astype(jnp.bfloat16)
@@ -157,7 +299,7 @@
     new_momentum = mu_decay * momentum + grad
     advance = (grad + mu_decay * new_momentum).astype(jnp.bfloat16)
     sizes = tuple(lax.axis_size(axis) for axis in SHARD_AXES)
-    whole = gather(advance, sizes, n_tensor)
+    whole = gather2(advance, sizes, n_tensor)
     wide = whole.astype(jnp.float32)
     frob = jnp.sqrt(jnp.sum(wide * wide)) + epsilon
     iterate = (wide / frob).astype(jnp.bfloat16)

time: 73.2 us -> 62.6 us (0.86)
  Pallas kernels: 50 us -> 39.4 us
    pallas_call x1, Pallas kernels: 50 us -> 39.4 us  [gather2(): pl.pallas_call(functools.partial(gather2_kernel, sizes, n_tensor), out_sh...]
where the time goes in v6:
time: 62.6 us; the launch traced here: 62.2 us
  Pallas kernels  39.4 us (63%)
  blocking collectives  9.01 us (14%)
  matrix products  7.76 us (12%)
  other arithmetic  4.69 us (7%)
  between operations  1.42 us (2%)
    pallas_call x1, Pallas kernels, gather2(): pl.pallas_call(functools.partial(gather2_kernel, sizes, n_tensor), out_sh...  39.4 us
    all_to_all x1, blocking collectives, on_device(): lax.all_to_all(pieces, 'tensor', split_axis=0, concat_axis=0, tiled=True)  9.01 us
    dot_general x3, matrix products, split_dot(): jnp.dot(both, jnp.concatenate([rhs, rhs], axis=0), preferred_element_type...  2.93 us
    dot_general x3, matrix products, polish(): squared = jnp.dot(squared_rows, gram, precision=lax.Precision.HIGH)  2.61 us
    reduce_sum x1, other arithmetic, on_device(): frob = jnp.sqrt(jnp.sum(wide * wide)) + epsilon  2.46 us
    dot_general x3, matrix products, on_device(): gram = jnp.dot(iterate, iterate.T, preferred_element_type=jnp.float32)  2.23 us
    convert_element_type x1, other arithmetic, on_device(): advance = (grad + mu_decay * new_momentum).astype(jnp.bfloat16)  1.4 us

profile of v6, /device:TPU:1, one launch (start us, length us, event | category | flops | bytes accessed | tf_op | source)
XLA Modules:
  0.0 62.2 jit_solution(843179505625353062)
XLA Ops:
  0.6 1.4 %add_convert_fusion.2 = (bf16[8,8,128]{2,1,0:T(8,128)(2,1)}, f32[8,8,128]{2,1,0:T(8,128)}) fusion(f32[8,8,128]{2,1,0:T(8,128)} %param.3, f32[8,8,128]{2,1,0:T(8,128)} %param.4), kind=kLoop, calls=%fused_computation.37 | loop fusion | flops 40960 | bytes 114688 | tf_op jit(solution)/shard_map/convert_element_type | solution.py:300
  2.0 39.4 %shard_map.58 = bf16[512,1024]{1,0:T(8,128)(2,1)} custom-call(bf16[8,8,128]{2,1,0:T(8,128)(2,1)} %get-tuple-element.11.adv_ref), custom_call_target="tpu_custom_call" | custom-call | tf_op jit(solution)/shard_map/pallas_call | solution.py:261
  41.4 0.0 copy-start
  41.4 2.5 %fusion = f32[]{:T(128)} fusion(bf16[512,1024]{1,0:T(8,128)(2,1)} %shard_map.58), kind=kLoop, calls=%fused_computation.2 | loop fusion | flops 1572863 | bytes 1048580 | tf_op jit(solution)/shard_map/reduce_sum | solution.py:304
  44.6 0.0 copy-done
  44.6 0.2 fusion.1
  44.8 0.7 %fusion.44 = f32[512,512]{0,1:T(8,128)S(1)} fusion(bf16[512,1024]{1,0:T(8,128)(2,1)S(1)} %fusion.1), kind=kOutput, calls=%fused_computation.48 | convolution fusion | flops 536870912 | bytes 2097152 | tf_op jit(solution)/shard_map/dot_general | solution.py:315
  45.5 1.1 %subtract_convert_fusion.1 = (bf16[512,512]{0,1:T(8,128)(2,1)S(1)}, bf16[512,512]{0,1:T(8,128)(2,1)S(1)}) fusion(f32[512,512]{0,1:T(8,128)S(1)} %fusion.44), kind=kOutput, calls=%fused_computation.34 | convolution fusion | flops 807141376 | bytes 2097152 | tf_op jit(solution)/shard_map/dot_general | solution.py:289
  46.7 1.3 %add_convert_fusion.1 = bf16[512,1024]{1,0:T(8,128)(2,1)S(1)} fusion(bf16[512,1024]{1,0:T(8,128)(2,1)S(1)} %fusion.1, bf16[512,512]{0,1:T(8,128)(2,1)S(1)} %get-tuple-element.9, bf16[512,512]{0,1:T(8,128)(2,1)S(1)} %get-tuple-element.10), kind=kOutput, calls=%fused_computation.17 | convolution fusion | flops 1082130432 | bytes 3145728 | tf_op jit(solution)/shard_map/dot_general | solution.py:284
  47.9 0.7 %fusion.45 = f32[512,512]{0,1:T(8,128)S(1)} fusion(bf16[512,1024]{1,0:T(8,128)(2,1)S(1)} %add_convert_fusion.1), kind=kOutput, calls=%fused_computation.49 | convolution fusion | flops 536870912 | bytes 2097152 | tf_op jit(solution)/shard_map/dot_general | solution.py:315
  48.7 1.1 %subtract_convert_fusion = (bf16[512,512]{0,1:T(8,128)(2,1)S(1)}, bf16[512,512]{0,1:T(8,128)(2,1)S(1)}) fusion(f32[512,512]{0,1:T(8,128)S(1)} %fusion.45), kind=kOutput, calls=%fused_computation.33 | convolution fusion | flops 807141376 | bytes 2097152 | tf_op jit(solution)/shard_map/dot_general | solution.py:289
  49.8 1.3 %add_convert_fusion = bf16[512,1024]{1,0:T(8,128)(2,1)S(1)} fusion(bf16[512,1024]{1,0:T(8,128)(2,1)S(1)} %add_convert_fusion.1, bf16[512,512]{0,1:T(8,128)(2,1)S(1)} %get-tuple-element.7, bf16[512,512]{0,1:T(8,128)(2,1)S(1)} %get-tuple-element.8), kind=kOutput, calls=%fused_computation.16 | convolution fusion | flops 1082130432 | bytes 3145728 | tf_op jit(solution)/shard_map/dot_general | solution.py:284
  51.1 0.7 %fusion.46 = f32[512,512]{1,0:T(8,128)S(1)} fusion(bf16[512,1024]{1,0:T(8,128)(2,1)S(1)} %add_convert_fusion), kind=kOutput, calls=%fused_computation.50 | convolution fusion | flops 536870912 | bytes 2097152 | tf_op jit(solution)/shard_map/dot_general | solution.py:315
  51.8 0.4 subtract_convert_fusion.2
  52.2 0.0 copy-start.1
  52.2 0.4 fusion.26
  52.6 9.0 %all_to_all.5 = bf16[8,8,128]{2,1,0:T(8,128)(2,1)S(1)} all-to-all(bf16[8,8,128]{2,1,0:T(8,128)(2,1)S(1)} %fusion.26), channel_id=1, replica_groups=mesh['sx'=4,'sz'=8,'sc'=2,'tensor'=8] {'tensor'}, dimensions={0} | all-to-all | bytes 32768 | tf_op jit(solution)/shard_map/all_to_all | solution.py:318
  61.6 0.0 copy-done.1
  61.6 0.6 %multiply_subtract_fusion = (f32[8,8,128]{2,1,0:T(8,128)}, f32[8,8,128]{2,1,0:T(8,128)}) fusion(f32[8,8,128]{2,1,0:T(8,128)S(1)} %copy-done.1, bf16[8,8,128]{2,1,0:T(8,128)(2,1)S(1)} %all_to_all.5), kind=kLoop, calls=%fused_computation.35 | loop fusion | flops 49152 | bytes 114688 | tf_op jit(solution)/shard_map/sub | solution.py:321
Async XLA Ops:
  41.4 3.2 %copy-start = (bf16[512,1024]{1,0:T(8,128)(2,1)S(1)}, bf16[512,1024]{1,0:T(8,128)(2,1)}, u32[]{:S(2)}) copy-start(bf16[512,1024]{1,0:T(8,128)(2,1)} %shard_map.58) | copy-start | bytes 3145732
  52.2 9.4 %copy-start.1 = (f32[8,8,128]{2,1,0:T(8,128)S(1)}, f32[8,8,128]{2,1,0:T(8,128)}, u32[]{:S(2)}) copy-start(f32[8,8,128]{2,1,0:T(8,128)} %param.5) | copy-start | bytes 98308

commit v7 on v6

--- a/solution.py
+++ b/solution.py
@@ -31,108 +31,6 @@
         coords.append(index % size)
         index = index // size
     return tuple(reversed(coords))
-
-
-def gather_kernel(sizes, n_tensor, adv_ref, out_ref, row_buf, whole_buf,
-                  send1, recv1, send2, recv2, local_sem):
-    mats, rows, cols = adv_ref.shape
-    n_shard = 1
-    for size in sizes:
-        n_shard *= size
-    here = tuple(lax.axis_index(a) for a in SHARD_AXES)
-    t = lax.axis_index("tensor")
-    me = 0
-    for axis, size in zip(SHARD_AXES, sizes):
-        me = me * size + lax.axis_index(axis)
-
-    def shard_peer(k):
-        return shard_coords(lax.rem(me + k, n_shard), sizes)
-
-    barrier = pltpu.get_barrier_semaphore()
-    for k in range(1, n_tensor):
-        pl.semaphore_signal(barrier, inc=1, device_id=here + (lax.rem(t + k, n_tensor),),
-                            device_id_type=MESH)
-
-    def greet(k, carry):
-        pl.semaphore_signal(barrier, inc=1, device_id=shard_peer(k) + (t,), device_id_type=MESH)
-        return carry
-
-    lax.fori_loop(1, n_shard, greet, 0)
-    pl.semaphore_wait(barrier, n_tensor - 1 + n_shard - 1)
-
-    my_cols = pl.ds(pl.multiple_of(t * cols, cols), cols)
-    own = pltpu.make_async_copy(adv_ref.at[t], row_buf.at[:, my_cols], local_sem)
-    own.start()
-    firsts = []
-    for k in range(1, n_tensor):
-        peer = lax.rem(t + k, n_tensor)
-        copy = pltpu.make_async_remote_copy(
-            src_ref=adv_ref.at[peer], dst_ref=row_buf.at[:, my_cols],
-            send_sem=send1.at[peer], recv_sem=recv1.at[t],
-            device_id=here + (peer,), device_id_type=MESH)
-        copy.start()
-        firsts.append(copy)
-    own.wait()
-    for k in range(1, n_tensor):
-        peer = lax.rem(t + k, n_tensor)
-        peer_cols = pl.ds(pl.multiple_of(peer * cols, cols), cols)
-        pltpu.make_async_remote_copy(
-            src_ref=adv_ref.at[t], dst_ref=row_buf.at[:, peer_cols],
-            send_sem=send1.at[peer], recv_sem=recv1.at[peer],
-            device_id=here + (peer,), device_id_type=MESH).wait_recv()
-        firsts[k - 1].wait_send()
-
-    my_rows = pl.ds(pl.multiple_of(me * rows, rows), rows)
-    own = pltpu.make_async_copy(row_buf, whole_buf.at[my_rows], local_sem)
-    own.start()
-
-    def send(k, carry):
-        peer = lax.rem(me + k, n_shard)
-        pltpu.make_async_remote_copy(
-            src_ref=row_buf, dst_ref=whole_buf.at[my_rows],
-            send_sem=send2.at[peer], recv_sem=recv2.at[me],
-            device_id=shard_coords(peer, sizes) + (t,), device_id_type=MESH).start()
-        return carry
-
-    lax.fori_loop(1, n_shard, send, 0)
-    own.wait()
-
-    def finish(k, carry):
-        peer = lax.rem(me + k, n_shard)
-        peer_rows = pl.ds(pl.multiple_of(peer * rows, rows), rows)
-        copy = pltpu.make_async_remote_copy(
-            src_ref=row_buf, dst_ref=whole_buf.at[peer_rows],
-            send_sem=send2.at[peer], recv_sem=recv2.at[peer],
-            device_id=shard_coords(peer, sizes) + (t,), device_id_type=MESH)
-        copy.wait_recv()
-        copy.wait_send()
-        return carry
-
-    lax.fori_loop(1, n_shard, finish, 0)
-    out_ref[...] = whole_buf[...]
-
-
-def gather(advance, sizes, n_tensor):
-    mats, rows, cols = advance.shape
-    n_shard = 1
-    for size in sizes:
-        n_shard *= size
-    return pl.pallas_call(
-        functools.partial(gather_kernel, sizes, n_tensor),
-        out_shape=jax.ShapeDtypeStruct((n_shard * rows, n_tensor * cols), advance.dtype),
-        in_specs=[pl.BlockSpec(memory_space=pltpu.VMEM)],
-        out_specs=pl.BlockSpec(memory_space=pltpu.VMEM),
-        scratch_shapes=[
-            pltpu.VMEM((rows, n_tensor * cols), advance.dtype),
-            pltpu.VMEM((n_shard * rows, n_tensor * cols), advance.dtype),
-            pltpu.SemaphoreType.DMA((n_tensor,)),
-            pltpu.SemaphoreType.DMA((n_tensor,)),
-            pltpu.SemaphoreType.DMA((n_shard,)),
-            pltpu.SemaphoreType.DMA((n_shard,)),
-            pltpu.SemaphoreType.DMA,
-        ],
-        compiler_params=pltpu.CompilerParams(collective_id=0, has_side_effects=True),
-    )(advance)
 
 
 def gather2_kernel(sizes, n_tensor, adv_ref, out_ref, row_buf, whole_buf,
@@ -277,6 +175,53 @@
     )(advance)
 
 
+def scatter_kernel(n_tensor, piece_ref, out_ref, out_buf, send_sem, recv_sem, local_sem):
+    here = tuple(lax.axis_index(a) for a in SHARD_AXES)
+    t = lax.axis_index("tensor")
+    barrier = pltpu.get_barrier_semaphore()
+    for k in range(1, n_tensor):
+        pl.semaphore_signal(barrier, inc=1, device_id=here + (lax.rem(t + k, n_tensor),),
+                            device_id_type=MESH)
+    pl.semaphore_wait(barrier, n_tensor - 1)
+    own = pltpu.make_async_copy(piece_ref.at[t], out_buf.at[t], local_sem)
+    own.start()
+    copies = []
+    for k in range(1, n_tensor):
+        peer = lax.rem(t + k, n_tensor)
+        copy = pltpu.make_async_remote_copy(
+            src_ref=piece_ref.at[peer], dst_ref=out_buf.at[t],
+            send_sem=send_sem.at[peer], recv_sem=recv_sem.at[t],
+            device_id=here + (peer,), device_id_type=MESH)
+        copy.start()
+        copies.append(copy)
+    own.wait()
+    for k in range(1, n_tensor):
+        peer = lax.rem(t + k, n_tensor)
+        pltpu.make_async_remote_copy(
+            src_ref=piece_ref.at[t], dst_ref=out_buf.at[peer],
+            send_sem=send_sem.at[peer], recv_sem=recv_sem.at[peer],
+            device_id=here + (peer,), device_id_type=MESH).wait_recv()
+        copies[k - 1].wait_send()
+    out_ref[...] = out_buf[...]
+
+
+def scatter(pieces):
+    n_tensor = pieces.shape[0]
+    return pl.pallas_call(
+        functools.partial(scatter_kernel, n_tensor),
+        out_shape=jax.ShapeDtypeStruct(pieces.shape, pieces.dtype),
+        in_specs=[pl.BlockSpec(memory_space=pltpu.VMEM)],
+        out_specs=pl.BlockSpec(memory_space=pltpu.VMEM),
+        scratch_shapes=[
+            pltpu.VMEM(pieces.shape, pieces.dtype),
+            pltpu.SemaphoreType.DMA((n_tensor,)),
+            pltpu.SemaphoreType.DMA((n_tensor,)),
+            pltpu.SemaphoreType.DMA,
+        ],
+        compiler_params=pltpu.CompilerParams(collective_id=1, has_side_effects=True),
+    )(pieces)
+
+
 def split_dot(wide_lhs, rhs):
     high = wide_lhs.astype(jnp.bfloat16)
     low = (wide_lhs - high.astype(jnp.float32)).astype(jnp.bfloat16)
@@ -315,7 +260,7 @@
         gram = jnp.dot(iterate, iterate.T, preferred_element_type=jnp.float32)
         iterate = polish(iterate, gram, mine if step == ITERS - 1 else None)
     pieces = iterate.reshape(rows_local, n_tensor, cols_local).transpose(1, 0, 2)
-    ortho = lax.all_to_all(pieces, "tensor", split_axis=0, concat_axis=0, tiled=True)
+    ortho = scatter(pieces)
     width = cols_local * n_tensor
     update = update_gain * math.sqrt(width) * ortho.astype(jnp.float32)
     new_weight = weight - learn_rate * (update + weight_decay * weight)

time: 62.6 us -> 63.6 us (1.016)
  blocking collectives: 9.01 us -> 0 us
  Pallas kernels: 39.4 us -> 47.9 us
  other arithmetic: 4.69 us -> 5.41 us
    all_to_all x1 -> x0, blocking collectives: 9.01 us -> none  [on_device(): lax.all_to_all(pieces, 'tensor', split_axis=0, concat_axis=0, tiled=True)]
    pallas_call x0 -> x1, Pallas kernels: none -> 8.57 us  [scatter(): pl.pallas_call(functools.partial(scatter_kernel, n_tensor), out_shape=jax...]
    sub x1, other arithmetic: 0.64 us -> 1.35 us  [on_device(): new_weight = weight - learn_rate * (update + weight_decay * weight)]
where the time goes in v7:
time: 63.6 us; the launch traced here: 63.2 us
  Pallas kernels  47.9 us (75%)
  matrix products  8.38 us (13%)
  other arithmetic  5.41 us (9%)
  between operations  1.43 us (2%)
    pallas_call x1, Pallas kernels, gather2(): pl.pallas_call(functools.partial(gather2_kernel, sizes, n_tensor), out_sh...  39.4 us
    pallas_call x1, Pallas kernels, scatter(): pl.pallas_call(functools.partial(scatter_kernel, n_tensor), out_shape=jax...  8.57 us
    dot_general x3, matrix products, split_dot(): jnp.dot(both, jnp.concatenate([rhs, rhs], axis=0), preferred_element_type...  3.54 us
    dot_general x3, matrix products, polish(): squared = jnp.dot(squared_rows, gram, precision=lax.Precision.HIGH)  2.61 us
    reduce_sum x1, other arithmetic, on_device(): frob = jnp.sqrt(jnp.sum(wide * wide)) + epsilon  2.46 us
    dot_general x3, matrix products, on_device(): gram = jnp.dot(iterate, iterate.T, preferred_element_type=jnp.float32)  2.23 us
    convert_element_type x1, other arithmetic, on_device(): advance = (grad + mu_decay * new_momentum).astype(jnp.bfloat16)  1.4 us
    sub x1, other arithmetic, on_device(): new_weight = weight - learn_rate * (update + weight_decay * weight)  1.35 us

profile of v7, /device:TPU:1, one launch (start us, length us, event | category | flops | bytes accessed | tf_op | source)
XLA Modules:
  0.0 63.2 jit_solution(6195760872246389539)
XLA Ops:
  0.6 1.4 %add_convert_fusion.2 = (bf16[8,8,128]{2,1,0:T(8,128)(2,1)}, f32[8,8,128]{2,1,0:T(8,128)}) fusion(f32[8,8,128]{2,1,0:T(8,128)} %param.3, f32[8,8,128]{2,1,0:T(8,128)} %param.4), kind=kLoop, calls=%fused_computation.37 | loop fusion | flops 40960 | bytes 114688 | tf_op jit(solution)/shard_map/convert_element_type | solution.py:245
  2.0 39.4 %shard_map.58 = bf16[512,1024]{1,0:T(8,128)(2,1)} custom-call(bf16[8,8,128]{2,1,0:T(8,128)(2,1)} %get-tuple-element.11.adv_ref), custom_call_target="tpu_custom_call" | custom-call | tf_op jit(solution)/shard_map/pallas_call | solution.py:159
  41.4 0.0 copy-start
  41.4 2.5 %fusion = f32[]{:T(128)} fusion(bf16[512,1024]{1,0:T(8,128)(2,1)} %shard_map.58), kind=kLoop, calls=%fused_computation.2 | loop fusion | flops 1572863 | bytes 1048580 | tf_op jit(solution)/shard_map/reduce_sum | solution.py:249
  44.6 0.0 copy-done
  44.6 0.2 fusion.1
  44.8 0.7 %fusion.44 = f32[512,512]{0,1:T(8,128)S(1)} fusion(bf16[512,1024]{1,0:T(8,128)(2,1)S(1)} %fusion.1), kind=kOutput, calls=%fused_computation.48 | convolution fusion | flops 536870912 | bytes 2097152 | tf_op jit(solution)/shard_map/dot_general | solution.py:260
  45.5 1.1 %subtract_convert_fusion.1 = (bf16[512,512]{0,1:T(8,128)(2,1)S(1)}, bf16[512,512]{0,1:T(8,128)(2,1)S(1)}) fusion(f32[512,512]{0,1:T(8,128)S(1)} %fusion.44), kind=kOutput, calls=%fused_computation.34 | convolution fusion | flops 807141376 | bytes 2097152 | tf_op jit(solution)/shard_map/dot_general | solution.py:234
  46.7 1.3 %add_convert_fusion.1 = bf16[512,1024]{1,0:T(8,128)(2,1)S(1)} fusion(bf16[512,1024]{1,0:T(8,128)(2,1)S(1)} %fusion.1, bf16[512,512]{0,1:T(8,128)(2,1)S(1)} %get-tuple-element.9, bf16[512,512]{0,1:T(8,128)(2,1)S(1)} %get-tuple-element.10), kind=kOutput, calls=%fused_computation.17 | convolution fusion | flops 1082130432 | bytes 3145728 | tf_op jit(solution)/shard_map/dot_general | solution.py:229
  47.9 0.7 %fusion.45 = f32[512,512]{0,1:T(8,128)S(1)} fusion(bf16[512,1024]{1,0:T(8,128)(2,1)S(1)} %add_convert_fusion.1), kind=kOutput, calls=%fused_computation.49 | convolution fusion | flops 536870912 | bytes 2097152 | tf_op jit(solution)/shard_map/dot_general | solution.py:260
  48.7 1.1 %subtract_convert_fusion = (bf16[512,512]{0,1:T(8,128)(2,1)S(1)}, bf16[512,512]{0,1:T(8,128)(2,1)S(1)}) fusion(f32[512,512]{0,1:T(8,128)S(1)} %fusion.45), kind=kOutput, calls=%fused_computation.33 | convolution fusion | flops 807141376 | bytes 2097152 | tf_op jit(solution)/shard_map/dot_general | solution.py:234
  49.8 1.3 %add_convert_fusion = bf16[512,1024]{1,0:T(8,128)(2,1)S(1)} fusion(bf16[512,1024]{1,0:T(8,128)(2,1)S(1)} %add_convert_fusion.1, bf16[512,512]{0,1:T(8,128)(2,1)S(1)} %get-tuple-element.7, bf16[512,512]{0,1:T(8,128)(2,1)S(1)} %get-tuple-element.8), kind=kOutput, calls=%fused_computation.16 | convolution fusion | flops 1082130432 | bytes 3145728 | tf_op jit(solution)/shard_map/dot_general | solution.py:229
  51.1 0.7 %fusion.46 = f32[512,512]{1,0:T(8,128)S(1)} fusion(bf16[512,1024]{1,0:T(8,128)(2,1)S(1)} %add_convert_fusion), kind=kOutput, calls=%fused_computation.50 | convolution fusion | flops 536870912 | bytes 2097152 | tf_op jit(solution)/shard_map/dot_general | solution.py:260
  51.8 0.4 subtract_convert_fusion.2
  52.2 0.0 copy-start.1
  52.2 1.0 %fusion.26.piece_ref = bf16[8,8,128]{2,1,0:T(8,128)(2,1)} fusion(bf16[512,1024]{1,0:T(8,128)(2,1)S(1)} %add_convert_fusion, bf16[8,512]{1,0:T(8,128)(2,1)S(1)} %get-tuple-element.5, bf16[8,512]{1,0:T(8,128)(2,1)S(1)} %get-tuple-element.6, s32[]{:T(128)S(6)} %select_n.4), kind=kOutput, calls=%fused_computation.24 | convolution fusion | flops 21037056 | bytes 1097732 | tf_op jit(solution)/shard_map/dot_general | solution.py:229
  53.2 8.6 %shard_map.59 = bf16[8,8,128]{2,1,0:T(8,128)(2,1)} custom-call(bf16[8,8,128]{2,1,0:T(8,128)(2,1)} %fusion.26.piece_ref), custom_call_target="tpu_custom_call" | custom-call | tf_op jit(solution)/shard_map/pallas_call | solution.py:210
  61.8 0.0 copy-done.1
  61.8 1.4 %multiply_subtract_fusion = (f32[8,8,128]{2,1,0:T(8,128)}, f32[8,8,128]{2,1,0:T(8,128)}) fusion(f32[8,8,128]{2,1,0:T(8,128)S(1)} %copy-done.1, bf16[8,8,128]{2,1,0:T(8,128)(2,1)} %shard_map.59), kind=kLoop, calls=%fused_computation.35 | loop fusion | flops 49152 | bytes 114688 | tf_op jit(solution)/shard_map/sub | solution.py:266
Async XLA Ops:
  41.4 3.2 %copy-start = (bf16[512,1024]{1,0:T(8,128)(2,1)S(1)}, bf16[512,1024]{1,0:T(8,128)(2,1)}, u32[]{:S(2)}) copy-start(bf16[512,1024]{1,0:T(8,128)(2,1)} %shard_map.58) | copy-start | bytes 3145732
  52.2 9.6 %copy-start.1 = (f32[8,8,128]{2,1,0:T(8,128)S(1)}, f32[8,8,128]{2,1,0:T(8,128)}, u32[]{:S(2)}) copy-start(f32[8,8,128]{2,1,0:T(8,128)} %param.5) | copy-start | bytes 98308

commit v8 on v7

--- a/solution.py
+++ b/solution.py
@@ -33,49 +33,33 @@
     return tuple(reversed(coords))
 
 
-def gather2_kernel(sizes, n_tensor, adv_ref, out_ref, row_buf, whole_buf,
-                   send1, recv1, send2, recv2, fwd, local_sem):
+def gather3_kernel(sizes, n_tensor, adv_ref, out_ref, row_buf, whole_buf,
+                   send1, recv1, send_x, recv_x, send_z, recv_z, send_c, recv_c, local_sem):
     mats, rows, cols = adv_ref.shape
-    n_core = sizes[-1]
-    n_chip = 1
-    for size in sizes[:-1]:
-        n_chip *= size
-    n_shard = n_chip * n_core
-    here = tuple(lax.axis_index(a) for a in SHARD_AXES)
+    n_x, n_z, n_c = sizes
+    x, z, c = (lax.axis_index(a) for a in SHARD_AXES)
+    here = (x, z, c)
     t = lax.axis_index("tensor")
-    me = 0
-    for axis, size in zip(SHARD_AXES, sizes):
-        me = me * size + lax.axis_index(axis)
-    core = lax.rem(me, n_core)
-    chip = me // n_core
-
-    def device(index):
-        return shard_coords(index, sizes) + (t,)
-
-    def chip_peer(k):
-        return lax.rem(chip + k, n_chip) * n_core + core
-
-    def sibling(j):
-        return chip * n_core + lax.rem(core + j, n_core)
+
+    def block(bx, bz, bc):
+        return (bc * n_z + bz) * n_x + bx
+
+    def span(first, count):
+        return pl.ds(pl.multiple_of(first * rows, rows), count * rows)
 
     barrier = pltpu.get_barrier_semaphore()
-    for k in range(1, n_tensor):
-        pl.semaphore_signal(barrier, inc=1, device_id=here + (lax.rem(t + k, n_tensor),),
-                            device_id_type=MESH)
-
-    def greet(k, carry):
-        pl.semaphore_signal(barrier, inc=1, device_id=device(chip_peer(k)), device_id_type=MESH)
-        return carry
-
-    lax.fori_loop(1, n_chip, greet, 0)
-    for j in range(1, n_core):
-        pl.semaphore_signal(barrier, inc=1, device_id=device(sibling(j)), device_id_type=MESH)
-    pl.semaphore_wait(barrier, n_tensor - 1 + n_chip - 1 + n_core - 1)
+    peers = [here + (lax.rem(t + k, n_tensor),) for k in range(1, n_tensor)]
+    peers += [(lax.rem(x + k, n_x), z, c, t) for k in range(1, n_x)]
+    peers += [(x, lax.rem(z + k, n_z), c, t) for k in range(1, n_z)]
+    peers += [(x, z, lax.rem(c + k, n_c), t) for k in range(1, n_c)]
+    for peer in peers:
+        pl.semaphore_signal(barrier, inc=1, device_id=peer, device_id_type=MESH)
+    pl.semaphore_wait(barrier, len(peers))
 
     my_cols = pl.ds(pl.multiple_of(t * cols, cols), cols)
     own = pltpu.make_async_copy(adv_ref.at[t], row_buf.at[:, my_cols], local_sem)
     own.start()
-    firsts = []
+    sent = []
     for k in range(1, n_tensor):
         peer = lax.rem(t + k, n_tensor)
         copy = pltpu.make_async_remote_copy(
@@ -83,7 +67,7 @@
             send_sem=send1.at[peer], recv_sem=recv1.at[t],
             device_id=here + (peer,), device_id_type=MESH)
         copy.start()
-        firsts.append(copy)
+        sent.append(copy)
     own.wait()
     for k in range(1, n_tensor):
         peer = lax.rem(t + k, n_tensor)
@@ -92,84 +76,90 @@
             src_ref=adv_ref.at[t], dst_ref=row_buf.at[:, peer_cols],
             send_sem=send1.at[peer], recv_sem=recv1.at[peer],
             device_id=here + (peer,), device_id_type=MESH).wait_recv()
-        firsts[k - 1].wait_send()
-
-    def rows_of(index):
-        return pl.ds(pl.multiple_of(index * rows, rows), rows)
-
-    def direct(dest):
-        return pltpu.make_async_remote_copy(
-            src_ref=row_buf, dst_ref=whole_buf.at[rows_of(me)],
-            send_sem=send2.at[dest], recv_sem=recv2.at[me],
-            device_id=device(dest), device_id_type=MESH)
-
-    def send(k, carry):
-        direct(chip_peer(k)).start()
-        return carry
-
-    lax.fori_loop(1, n_chip, send, 0)
-    for j in range(1, n_core):
-        direct(sibling(j)).start()
-    own = pltpu.make_async_copy(row_buf, whole_buf.at[rows_of(me)], local_sem)
+    for copy in sent:
+        copy.wait_send()
+
+    mine = span(block(x, z, c), 1)
+    own = pltpu.make_async_copy(row_buf, whole_buf.at[mine], local_sem)
     own.start()
-
-    def forward(source, dest):
-        return pltpu.make_async_remote_copy(
-            src_ref=whole_buf.at[rows_of(source)], dst_ref=whole_buf.at[rows_of(source)],
-            send_sem=fwd.at[source], recv_sem=recv2.at[source],
-            device_id=device(dest), device_id_type=MESH)
-
-    def relay(k, carry):
-        source = chip_peer(k)
-        pltpu.make_async_remote_copy(
-            src_ref=row_buf, dst_ref=whole_buf.at[rows_of(source)],
-            send_sem=send2.at[source], recv_sem=recv2.at[source],
-            device_id=device(source), device_id_type=MESH).wait_recv()
-        for j in range(1, n_core):
-            forward(source, sibling(j)).start()
-        return carry
-
-    lax.fori_loop(1, n_chip, relay, 0)
+    sent = []
+    for k in range(1, n_x):
+        peer = lax.rem(x + k, n_x)
+        copy = pltpu.make_async_remote_copy(
+            src_ref=row_buf, dst_ref=whole_buf.at[mine],
+            send_sem=send_x.at[peer], recv_sem=recv_x.at[x],
+            device_id=(peer, z, c, t), device_id_type=MESH)
+        copy.start()
+        sent.append(copy)
     own.wait()
-
-    def settle(k, carry):
-        source = chip_peer(k)
-        direct(source).wait_send()
-        for j in range(1, n_core):
-            forward(source, sibling(j)).wait_send()
-            other = source - core + lax.rem(core + j, n_core)
-            forward(other, sibling(j)).wait_recv()
-        return carry
-
-    lax.fori_loop(1, n_chip, settle, 0)
-    for j in range(1, n_core):
-        direct(sibling(j)).wait_send()
-        pltpu.make_async_remote_copy(
-            src_ref=row_buf, dst_ref=whole_buf.at[rows_of(sibling(j))],
-            send_sem=send2.at[sibling(j)], recv_sem=recv2.at[sibling(j)],
-            device_id=device(sibling(j)), device_id_type=MESH).wait_recv()
+    for k in range(1, n_x):
+        peer = lax.rem(x + k, n_x)
+        pltpu.make_async_remote_copy(
+            src_ref=row_buf, dst_ref=whole_buf.at[span(block(peer, z, c), 1)],
+            send_sem=send_x.at[peer], recv_sem=recv_x.at[peer],
+            device_id=(peer, z, c, t), device_id_type=MESH).wait_recv()
+    for copy in sent:
+        copy.wait_send()
+
+    strip = span(block(0, z, c), n_x)
+    sent = []
+    for k in range(1, n_z):
+        peer = lax.rem(z + k, n_z)
+        copy = pltpu.make_async_remote_copy(
+            src_ref=whole_buf.at[strip], dst_ref=whole_buf.at[strip],
+            send_sem=send_z.at[peer], recv_sem=recv_z.at[z],
+            device_id=(x, peer, c, t), device_id_type=MESH)
+        copy.start()
+        sent.append(copy)
+    for k in range(1, n_z):
+        peer = lax.rem(z + k, n_z)
+        other = span(block(0, peer, c), n_x)
+        pltpu.make_async_remote_copy(
+            src_ref=whole_buf.at[other], dst_ref=whole_buf.at[other],
+            send_sem=send_z.at[peer], recv_sem=recv_z.at[peer],
+            device_id=(x, peer, c, t), device_id_type=MESH).wait_recv()
+    for copy in sent:
+        copy.wait_send()
+
+    half = span(block(0, 0, c), n_z * n_x)
+    sent = []
+    for k in range(1, n_c):
+        peer = lax.rem(c + k, n_c)
+        copy = pltpu.make_async_remote_copy(
+            src_ref=whole_buf.at[half], dst_ref=whole_buf.at[half],
+            send_sem=send_c.at[peer], recv_sem=recv_c.at[c],
+            device_id=(x, z, peer, t), device_id_type=MESH)
+        copy.start()
+        sent.append(copy)
+    for k in range(1, n_c):
+        peer = lax.rem(c + k, n_c)
+        other = span(block(0, 0, peer), n_z * n_x)
+        pltpu.make_async_remote_copy(
+            src_ref=whole_buf.at[other], dst_ref=whole_buf.at[other],
+            send_sem=send_c.at[peer], recv_sem=recv_c.at[peer],
+            device_id=(x, z, peer, t), device_id_type=MESH).wait_recv()
+    for copy in sent:
+        copy.wait_send()
     out_ref[...] = whole_buf[...]
 
 
-def gather2(advance, sizes, n_tensor):
+def gather3(advance, sizes, n_tensor):
     mats, rows, cols = advance.shape
-    n_shard = 1
-    for size in sizes:
-        n_shard *= size
+    n_x, n_z, n_c = sizes
+    DMA = pltpu.SemaphoreType.DMA
     return pl.pallas_call(
-        functools.partial(gather2_kernel, sizes, n_tensor),
-        out_shape=jax.ShapeDtypeStruct((n_shard * rows, n_tensor * cols), advance.dtype),
+        functools.partial(gather3_kernel, sizes, n_tensor),
+        out_shape=jax.ShapeDtypeStruct((n_x * n_z * n_c * rows, n_tensor * cols), advance.dtype),
         in_specs=[pl.BlockSpec(memory_space=pltpu.VMEM)],
         out_specs=pl.BlockSpec(memory_space=pltpu.VMEM),
         scratch_shapes=[
             pltpu.VMEM((rows, n_tensor * cols), advance.dtype),
-            pltpu.VMEM((n_shard * rows, n_tensor * cols), advance.dtype),
-            pltpu.SemaphoreType.DMA((n_tensor,)),
-            pltpu.SemaphoreType.DMA((n_tensor,)),
-            pltpu.SemaphoreType.DMA((n_shard,)),
-            pltpu.SemaphoreType.DMA((n_shard,)),
-            pltpu.SemaphoreType.DMA((n_shard,)),
-            pltpu.SemaphoreType.DMA,
+            pltpu.VMEM((n_x * n_z * n_c * rows, n_tensor * cols), advance.dtype),
+            DMA((n_tensor,)), DMA((n_tensor,)),
+            DMA((n_x,)), DMA((n_x,)),
+            DMA((n_z,)), DMA((n_z,)),
+            DMA((n_c,)), DMA((n_c,)),
+            DMA,
         ],
         compiler_params=pltpu.CompilerParams(collective_id=0, has_side_effects=True),
     )(advance)
@@ -244,12 +234,12 @@
     new_momentum = mu_decay * momentum + grad
     advance = (grad + mu_decay * new_momentum).astype(jnp.bfloat16)
     sizes = tuple(lax.axis_size(axis) for axis in SHARD_AXES)
-    whole = gather2(advance, sizes, n_tensor)
+    whole = gather3(advance, sizes, n_tensor)
     wide = whole.astype(jnp.float32)
     frob = jnp.sqrt(jnp.sum(wide * wide)) + epsilon
     iterate = (wide / frob).astype(jnp.bfloat16)
     block = 0
-    for axis in SHARD_AXES:
+    for axis in reversed(SHARD_AXES):
         block = block * lax.axis_size(axis) + lax.axis_index(axis)
     start = block * rows_local
 

time: 63.6 us -> 63 us (level)
  no operation moved by 1% of the time
where the time goes in v8:
time: 63 us; the launch traced here: 62.6 us
  Pallas kernels  47.4 us (75%)
  matrix products  8.37 us (13%)
  other arithmetic  5.41 us (9%)
  between operations  1.43 us (2%)
    pallas_call x1, Pallas kernels, gather3(): pl.pallas_call(functools.partial(gather3_kernel, sizes, n_tensor), out_sh...  38.8 us
    pallas_call x1, Pallas kernels, scatter(): pl.pallas_call(functools.partial(scatter_kernel, n_tensor), out_shape=jax...  8.57 us
    dot_general x3, matrix products, split_dot(): jnp.dot(both, jnp.concatenate([rhs, rhs], axis=0), preferred_element_type...  3.54 us
    dot_general x3, matrix products, polish(): squared = jnp.dot(squared_rows, gram, precision=lax.Precision.HIGH)  2.61 us
    reduce_sum x1, other arithmetic, on_device(): frob = jnp.sqrt(jnp.sum(wide * wide)) + epsilon  2.46 us
    dot_general x3, matrix products, on_device(): gram = jnp.dot(iterate, iterate.T, preferred_element_type=jnp.float32)  2.23 us
    convert_element_type x1, other arithmetic, on_device(): advance = (grad + mu_decay * new_momentum).astype(jnp.bfloat16)  1.4 us
    sub x1, other arithmetic, on_device(): new_weight = weight - learn_rate * (update + weight_decay * weight)  1.35 us

profile of v8, /device:TPU:1, one launch (start us, length us, event | category | flops | bytes accessed | tf_op | source)
XLA Modules:
  0.0 62.6 jit_solution(4760967151915572232)
XLA Ops:
  0.6 1.4 %add_convert_fusion.2 = (bf16[8,8,128]{2,1,0:T(8,128)(2,1)}, f32[8,8,128]{2,1,0:T(8,128)}) fusion(f32[8,8,128]{2,1,0:T(8,128)} %param.3, f32[8,8,128]{2,1,0:T(8,128)} %param.4), kind=kLoop, calls=%fused_computation.37 | loop fusion | flops 40960 | bytes 114688 | tf_op jit(solution)/shard_map/convert_element_type | solution.py:235
  2.0 38.8 %shard_map.58 = bf16[512,1024]{1,0:T(8,128)(2,1)} custom-call(bf16[8,8,128]{2,1,0:T(8,128)(2,1)} %get-tuple-element.11.adv_ref), custom_call_target="tpu_custom_call" | custom-call | tf_op jit(solution)/shard_map/pallas_call | solution.py:150
  40.8 0.0 copy-start
  40.8 2.5 %fusion = f32[]{:T(128)} fusion(bf16[512,1024]{1,0:T(8,128)(2,1)} %shard_map.58), kind=kLoop, calls=%fused_computation.2 | loop fusion | flops 1572863 | bytes 1048580 | tf_op jit(solution)/shard_map/reduce_sum | solution.py:239
  44.0 0.0 copy-done
  44.0 0.2 fusion.1
  44.2 0.7 %fusion.44 = f32[512,512]{0,1:T(8,128)S(1)} fusion(bf16[512,1024]{1,0:T(8,128)(2,1)S(1)} %fusion.1), kind=kOutput, calls=%fused_computation.48 | convolution fusion | flops 536870912 | bytes 2097152 | tf_op jit(solution)/shard_map/dot_general | solution.py:250
  44.9 1.1 %subtract_convert_fusion.1 = (bf16[512,512]{0,1:T(8,128)(2,1)S(1)}, bf16[512,512]{0,1:T(8,128)(2,1)S(1)}) fusion(f32[512,512]{0,1:T(8,128)S(1)} %fusion.44), kind=kOutput, calls=%fused_computation.34 | convolution fusion | flops 807141376 | bytes 2097152 | tf_op jit(solution)/shard_map/dot_general | solution.py:224
  46.1 1.3 %add_convert_fusion.1 = bf16[512,1024]{1,0:T(8,128)(2,1)S(1)} fusion(bf16[512,1024]{1,0:T(8,128)(2,1)S(1)} %fusion.1, bf16[512,512]{0,1:T(8,128)(2,1)S(1)} %get-tuple-element.9, bf16[512,512]{0,1:T(8,128)(2,1)S(1)} %get-tuple-element.10), kind=kOutput, calls=%fused_computation.17 | convolution fusion | flops 1082130432 | bytes 3145728 | tf_op jit(solution)/shard_map/dot_general | solution.py:219
  47.4 0.7 %fusion.45 = f32[512,512]{0,1:T(8,128)S(1)} fusion(bf16[512,1024]{1,0:T(8,128)(2,1)S(1)} %add_convert_fusion.1), kind=kOutput, calls=%fused_computation.49 | convolution fusion | flops 536870912 | bytes 2097152 | tf_op jit(solution)/shard_map/dot_general | solution.py:250
  48.1 1.1 %subtract_convert_fusion = (bf16[512,512]{0,1:T(8,128)(2,1)S(1)}, bf16[512,512]{0,1:T(8,128)(2,1)S(1)}) fusion(f32[512,512]{0,1:T(8,128)S(1)} %fusion.45), kind=kOutput, calls=%fused_computation.33 | convolution fusion | flops 807141376 | bytes 2097152 | tf_op jit(solution)/shard_map/dot_general | solution.py:224
  49.2 1.3 %add_convert_fusion = bf16[512,1024]{1,0:T(8,128)(2,1)S(1)} fusion(bf16[512,1024]{1,0:T(8,128)(2,1)S(1)} %add_convert_fusion.1, bf16[512,512]{0,1:T(8,128)(2,1)S(1)} %get-tuple-element.7, bf16[512,512]{0,1:T(8,128)(2,1)S(1)} %get-tuple-element.8), kind=kOutput, calls=%fused_computation.16 | convolution fusion | flops 1082130432 | bytes 3145728 | tf_op jit(solution)/shard_map/dot_general | solution.py:219
  50.5 0.7 %fusion.46 = f32[512,512]{1,0:T(8,128)S(1)} fusion(bf16[512,1024]{1,0:T(8,128)(2,1)S(1)} %add_convert_fusion), kind=kOutput, calls=%fused_computation.50 | convolution fusion | flops 536870912 | bytes 2097152 | tf_op jit(solution)/shard_map/dot_general | solution.py:250
  51.3 0.4 subtract_convert_fusion.2
  51.6 0.0 copy-start.1
  51.6 1.0 %fusion.26.piece_ref = bf16[8,8,128]{2,1,0:T(8,128)(2,1)} fusion(bf16[512,1024]{1,0:T(8,128)(2,1)S(1)} %add_convert_fusion, bf16[8,512]{1,0:T(8,128)(2,1)S(1)} %get-tuple-element.5, bf16[8,512]{1,0:T(8,128)(2,1)S(1)} %get-tuple-element.6, s32[]{:T(128)S(6)} %select_n.4), kind=kOutput, calls=%fused_computation.24 | convolution fusion | flops 21037056 | bytes 1097732 | tf_op jit(solution)/shard_map/dot_general | solution.py:219
  52.6 8.6 %shard_map.59 = bf16[8,8,128]{2,1,0:T(8,128)(2,1)} custom-call(bf16[8,8,128]{2,1,0:T(8,128)(2,1)} %fusion.26.piece_ref), custom_call_target="tpu_custom_call" | custom-call | tf_op jit(solution)/shard_map/pallas_call | solution.py:200
  61.2 0.0 copy-done.1
  61.2 1.4 %multiply_subtract_fusion = (f32[8,8,128]{2,1,0:T(8,128)}, f32[8,8,128]{2,1,0:T(8,128)}) fusion(f32[8,8,128]{2,1,0:T(8,128)S(1)} %copy-done.1, bf16[8,8,128]{2,1,0:T(8,128)(2,1)} %shard_map.59), kind=kLoop, calls=%fused_computation.35 | loop fusion | flops 49152 | bytes 114688 | tf_op jit(solution)/shard_map/sub | solution.py:256
Async XLA Ops:
  40.8 3.2 %copy-start = (bf16[512,1024]{1,0:T(8,128)(2,1)S(1)}, bf16[512,1024]{1,0:T(8,128)(2,1)}, u32[]{:S(2)}) copy-start(bf16[512,1024]{1,0:T(8,128)(2,1)} %shard_map.58) | copy-start | bytes 3145732
  51.6 9.6 %copy-start.1 = (f32[8,8,128]{2,1,0:T(8,128)S(1)}, f32[8,8,128]{2,1,0:T(8,128)}, u32[]{:S(2)}) copy-start(f32[8,8,128]{2,1,0:T(8,128)} %param.5) | copy-start | bytes 98308

commit v9 on v8

--- a/solution.py
+++ b/solution.py
@@ -33,7 +33,7 @@
     return tuple(reversed(coords))
 
 
-def gather3_kernel(sizes, n_tensor, adv_ref, out_ref, row_buf, whole_buf,
+def gather3_kernel(sizes, n_tensor, adv_ref, out_ref, square_ref, row_buf, whole_buf,
                    send1, recv1, send_x, recv_x, send_z, recv_z, send_c, recv_c, local_sem):
     mats, rows, cols = adv_ref.shape
     n_x, n_z, n_c = sizes
@@ -142,6 +142,14 @@
         copy.wait_send()
     out_ref[...] = whole_buf[...]
 
+    def square(i, total):
+        piece = whole_buf[pl.ds(pl.multiple_of(i * rows, rows), rows), :].astype(jnp.float32)
+        return total + piece * piece
+
+    total = lax.fori_loop(0, n_x * n_z * n_c, square,
+                          jnp.zeros((rows, n_tensor * cols), jnp.float32))
+    square_ref[...] = jnp.broadcast_to(jnp.sum(total), square_ref.shape)
+
 
 def gather3(advance, sizes, n_tensor):
     mats, rows, cols = advance.shape
@@ -149,9 +157,12 @@
     DMA = pltpu.SemaphoreType.DMA
     return pl.pallas_call(
         functools.partial(gather3_kernel, sizes, n_tensor),
-        out_shape=jax.ShapeDtypeStruct((n_x * n_z * n_c * rows, n_tensor * cols), advance.dtype),
+        out_shape=(
+            jax.ShapeDtypeStruct((n_x * n_z * n_c * rows, n_tensor * cols), advance.dtype),
+            jax.ShapeDtypeStruct((8, 128), jnp.float32),
+        ),
         in_specs=[pl.BlockSpec(memory_space=pltpu.VMEM)],
-        out_specs=pl.BlockSpec(memory_space=pltpu.VMEM),
+        out_specs=(pl.BlockSpec(memory_space=pltpu.VMEM), pl.BlockSpec(memory_space=pltpu.VMEM)),
         scratch_shapes=[
             pltpu.VMEM((rows, n_tensor * cols), advance.dtype),
             pltpu.VMEM((n_x * n_z * n_c * rows, n_tensor * cols), advance.dtype),
@@ -234,9 +245,9 @@
     new_momentum = mu_decay * momentum + grad
     advance = (grad + mu_decay * new_momentum).astype(jnp.bfloat16)
     sizes = tuple(lax.axis_size(axis) for axis in SHARD_AXES)
-    whole = gather3(advance, sizes, n_tensor)
+    whole, squares = gather3(advance, sizes, n_tensor)
     wide = whole.astype(jnp.float32)
-    frob = jnp.sqrt(jnp.sum(wide * wide)) + epsilon
+    frob = jnp.sqrt(squares[0, 0]) + epsilon
     iterate = (wide / frob).astype(jnp.bfloat16)
     block = 0
     for axis in reversed(SHARD_AXES):

time: 63 us -> 63.5 us (level)
  other arithmetic: 5.41 us -> 4.19 us
  local copies, waits for them, and re-layouts: 0.01 us -> 1.2 us
    reduce_sum x1 -> x0, other arithmetic: 2.46 us -> none  [on_device(): frob = jnp.sqrt(jnp.sum(wide * wide)) + epsilon]
    convert_element_type x1, other arithmetic: 0.2 us -> 1.44 us  [on_device(): iterate = (wide / frob).astype(jnp.bfloat16)]
    slice x0 -> x1, local copies, waits for them, and re-layouts: none -> 1.19 us  [on_device(): frob = jnp.sqrt(squares[0, 0]) + epsilon]
where the time goes in v9:
time: 63.5 us; the launch traced here: 63 us
  Pallas kernels  47.8 us (75%)
  matrix products  8.38 us (13%)
  other arithmetic  4.19 us (7%)
  between operations  1.41 us (2%)
  local copies, waits for them, and re-layouts  1.2 us (2%)
    pallas_call x1, Pallas kernels, gather3(): pl.pallas_call(functools.partial(gather3_kernel, sizes, n_tensor), out_sh...  39.3 us
    pallas_call x1, Pallas kernels, scatter(): pl.pallas_call(functools.partial(scatter_kernel, n_tensor), out_shape=jax...  8.58 us
    dot_general x3, matrix products, split_dot(): jnp.dot(both, jnp.concatenate([rhs, rhs], axis=0), preferred_element_type...  3.54 us
    dot_general x3, matrix products, polish(): squared = jnp.dot(squared_rows, gram, precision=lax.Precision.HIGH)  2.61 us
    dot_general x3, matrix products, on_device(): gram = jnp.dot(iterate, iterate.T, preferred_element_type=jnp.float32)  2.23 us
    convert_element_type x1, other arithmetic, on_device(): iterate = (wide / frob).astype(jnp.bfloat16)  1.44 us
    convert_element_type x1, other arithmetic, on_device(): advance = (grad + mu_decay * new_momentum).astype(jnp.bfloat16)  1.4 us
    sub x1, other arithmetic, on_device(): new_weight = weight - learn_rate * (update + weight_decay * weight)  1.35 us

profile of v9, /device:TPU:1, one launch (start us, length us, event | category | flops | bytes accessed | tf_op | source)
XLA Modules:
  0.0 63.0 jit_solution(5430902167848561419)
XLA Ops:
  0.6 1.4 %add_convert_fusion.2 = (bf16[8,8,128]{2,1,0:T(8,128)(2,1)}, f32[8,8,128]{2,1,0:T(8,128)}) fusion(f32[8,8,128]{2,1,0:T(8,128)} %param.3, f32[8,8,128]{2,1,0:T(8,128)} %param.4), kind=kLoop, calls=%fused_computation.34 | loop fusion | flops 40960 | bytes 114688 | tf_op jit(solution)/shard_map/convert_element_type | solution.py:246
  2.0 39.3 %shard_map.58 = (bf16[512,1024]{1,0:T(8,128)(2,1)}, f32[8,128]{1,0:T(8,128)}) custom-call(bf16[8,8,128]{2,1,0:T(8,128)(2,1)} %get-tuple-element.15.adv_ref), custom_call_target="tpu_custom_call" | custom-call | tf_op jit(solution)/shard_map/pallas_call | solution.py:158
  41.3 1.2 %slice.3 = f32[1,1]{1,0:T(1,128)} slice(f32[8,128]{1,0:T(8,128)} %get-tuple-element.6), slice={[0:1], [0:1]} | slice | bytes 8 | tf_op jit(solution)/shard_map/slice | solution.py:250
  43.2 1.4 %divide_convert_fusion = bf16[512,1024]{1,0:T(8,128)(2,1)S(1)} fusion(bf16[512,1024]{1,0:T(8,128)(2,1)} %get-tuple-element.5, f32[]{:T(128)} %bitcast), kind=kLoop, calls=%fused_computation.14 | loop fusion | flops 1572864 | bytes 2097156 | tf_op jit(solution)/shard_map/convert_element_type | solution.py:251
  44.6 0.7 %fusion.42 = f32[512,512]{0,1:T(8,128)S(1)} fusion(bf16[512,1024]{1,0:T(8,128)(2,1)S(1)} %divide_convert_fusion), kind=kOutput, calls=%fused_computation.45 | convolution fusion | flops 536870912 | bytes 2097152 | tf_op jit(solution)/shard_map/dot_general | solution.py:261
  45.4 1.1 %subtract_convert_fusion.1 = (bf16[512,512]{0,1:T(8,128)(2,1)S(1)}, bf16[512,512]{0,1:T(8,128)(2,1)S(1)}) fusion(f32[512,512]{0,1:T(8,128)S(1)} %fusion.42), kind=kOutput, calls=%fused_computation.31 | convolution fusion | flops 807141376 | bytes 2097152 | tf_op jit(solution)/shard_map/dot_general | solution.py:235
  46.5 1.3 %add_convert_fusion.1 = bf16[512,1024]{1,0:T(8,128)(2,1)S(1)} fusion(bf16[512,1024]{1,0:T(8,128)(2,1)S(1)} %divide_convert_fusion, bf16[512,512]{0,1:T(8,128)(2,1)S(1)} %get-tuple-element.13, bf16[512,512]{0,1:T(8,128)(2,1)S(1)} %get-tuple-element.14), kind=kOutput, calls=%fused_computation.13 | convolution fusion | flops 1082130432 | bytes 3145728 | tf_op jit(solution)/shard_map/dot_general | solution.py:230
  47.8 0.7 %fusion.43 = f32[512,512]{0,1:T(8,128)S(1)} fusion(bf16[512,1024]{1,0:T(8,128)(2,1)S(1)} %add_convert_fusion.1), kind=kOutput, calls=%fused_computation.46 | convolution fusion | flops 536870912 | bytes 2097152 | tf_op jit(solution)/shard_map/dot_general | solution.py:261
  48.5 1.1 %subtract_convert_fusion = (bf16[512,512]{0,1:T(8,128)(2,1)S(1)}, bf16[512,512]{0,1:T(8,128)(2,1)S(1)}) fusion(f32[512,512]{0,1:T(8,128)S(1)} %fusion.43), kind=kOutput, calls=%fused_computation.30 | convolution fusion | flops 807141376 | bytes 2097152 | tf_op jit(solution)/shard_map/dot_general | solution.py:235
  49.7 1.3 %add_convert_fusion = bf16[512,1024]{1,0:T(8,128)(2,1)S(1)} fusion(bf16[512,1024]{1,0:T(8,128)(2,1)S(1)} %add_convert_fusion.1, bf16[512,512]{0,1:T(8,128)(2,1)S(1)} %get-tuple-element.11, bf16[512,512]{0,1:T(8,128)(2,1)S(1)} %get-tuple-element.12), kind=kOutput, calls=%fused_computation.12 | convolution fusion | flops 1082130432 | bytes 3145728 | tf_op jit(solution)/shard_map/dot_general | solution.py:230
  50.9 0.7 %fusion.44 = f32[512,512]{1,0:T(8,128)S(1)} fusion(bf16[512,1024]{1,0:T(8,128)(2,1)S(1)} %add_convert_fusion), kind=kOutput, calls=%fused_computation.47 | convolution fusion | flops 536870912 | bytes 2097152 | tf_op jit(solution)/shard_map/dot_general | solution.py:261
  51.7 0.4 subtract_convert_fusion.2
  52.1 0.0 copy-start
  52.1 1.0 %fusion.24.piece_ref = bf16[8,8,128]{2,1,0:T(8,128)(2,1)} fusion(bf16[512,1024]{1,0:T(8,128)(2,1)S(1)} %add_convert_fusion, bf16[8,512]{1,0:T(8,128)(2,1)S(1)} %get-tuple-element.9, bf16[8,512]{1,0:T(8,128)(2,1)S(1)} %get-tuple-element.10, s32[]{:T(128)S(6)} %select_n.4), kind=kOutput, calls=%fused_computation.21 | convolution fusion | flops 21037056 | bytes 1097732 | tf_op jit(solution)/shard_map/dot_general | solution.py:230
  53.1 8.6 %shard_map.59 = bf16[8,8,128]{2,1,0:T(8,128)(2,1)} custom-call(bf16[8,8,128]{2,1,0:T(8,128)(2,1)} %fusion.24.piece_ref), custom_call_target="tpu_custom_call" | custom-call | tf_op jit(solution)/shard_map/pallas_call | solution.py:211
  61.6 0.0 copy-done
  61.7 1.4 %multiply_subtract_fusion = (f32[8,8,128]{2,1,0:T(8,128)}, f32[8,8,128]{2,1,0:T(8,128)}) fusion(f32[8,8,128]{2,1,0:T(8,128)S(1)} %copy-done, bf16[8,8,128]{2,1,0:T(8,128)(2,1)} %shard_map.59), kind=kLoop, calls=%fused_computation.32 | loop fusion | flops 49152 | bytes 114688 | tf_op jit(solution)/shard_map/sub | solution.py:267
Async XLA Ops:
  52.1 9.6 %copy-start = (f32[8,8,128]{2,1,0:T(8,128)S(1)}, f32[8,8,128]{2,1,0:T(8,128)}, u32[]{:S(2)}) copy-start(f32[8,8,128]{2,1,0:T(8,128)} %param.5) | copy-start | bytes 98308

commit v10 on v9

--- a/solution.py
+++ b/solution.py
@@ -239,6 +239,81 @@
     return fresh.astype(jnp.bfloat16)
 
 
+def two_part(wide):
+    high = wide.astype(jnp.bfloat16)
+    return high, (wide - high.astype(jnp.float32)).astype(jnp.bfloat16)
+
+
+def finish_kernel(sizes, n_tensor, x_ref, out_ref, piece_buf, out_buf, send_sem, recv_sem, local_sem):
+    n_x, n_z, n_c = sizes
+    x, z, c = (lax.axis_index(a) for a in SHARD_AXES)
+    here = (x, z, c)
+    t = lax.axis_index("tensor")
+    _, rows, cols = piece_buf.shape
+    barrier = pltpu.get_barrier_semaphore()
+    for k in range(1, n_tensor):
+        pl.semaphore_signal(barrier, inc=1, device_id=here + (lax.rem(t + k, n_tensor),),
+                            device_id_type=MESH)
+    block = (c * n_z + z) * n_x + x
+    head = x_ref[pl.ds(pl.multiple_of(block * rows, rows), rows), :]
+    full = x_ref[...]
+    by_rows = (((1,), (1,)), ((), ()))
+    gram = lax.dot_general(head, full, by_rows, preferred_element_type=jnp.float32)
+    high, low = two_part(gram)
+    across = (jnp.dot(high, full, preferred_element_type=jnp.float32)
+              + jnp.dot(low, full, preferred_element_type=jnp.float32))
+    high, low = two_part(across)
+    squared = (lax.dot_general(high, full, by_rows, preferred_element_type=jnp.float32)
+               + lax.dot_general(low, full, by_rows, preferred_element_type=jnp.float32))
+    poly = second_coef * gram + third_coef * squared
+    high, low = two_part(poly)
+    mixed = (jnp.dot(high, full, preferred_element_type=jnp.float32)
+             + jnp.dot(low, full, preferred_element_type=jnp.float32))
+    fresh = (first_coef * head.astype(jnp.float32) + mixed).astype(jnp.bfloat16)
+    for j in range(n_tensor):
+        piece_buf[j] = fresh[:, j * cols:(j + 1) * cols]
+    pl.semaphore_wait(barrier, n_tensor - 1)
+    own = pltpu.make_async_copy(piece_buf.at[t], out_buf.at[t], local_sem)
+    own.start()
+    copies = []
+    for k in range(1, n_tensor):
+        peer = lax.rem(t + k, n_tensor)
+        copy = pltpu.make_async_remote_copy(
+            src_ref=piece_buf.at[peer], dst_ref=out_buf.at[t],
+            send_sem=send_sem.at[peer], recv_sem=recv_sem.at[t],
+            device_id=here + (peer,), device_id_type=MESH)
+        copy.start()
+        copies.append(copy)
+    own.wait()
+    for k in range(1, n_tensor):
+        peer = lax.rem(t + k, n_tensor)
+        pltpu.make_async_remote_copy(
+            src_ref=piece_buf.at[t], dst_ref=out_buf.at[peer],
+            send_sem=send_sem.at[peer], recv_sem=recv_sem.at[peer],
+            device_id=here + (peer,), device_id_type=MESH).wait_recv()
+        copies[k - 1].wait_send()
+    out_ref[...] = out_buf[...]
+
+
+def finish(iterate, sizes, n_tensor, rows):
+    cols = iterate.shape[1] // n_tensor
+    shape = (n_tensor, rows, cols)
+    return pl.pallas_call(
+        functools.partial(finish_kernel, sizes, n_tensor),
+        out_shape=jax.ShapeDtypeStruct(shape, iterate.dtype),
+        in_specs=[pl.BlockSpec(memory_space=pltpu.VMEM)],
+        out_specs=pl.BlockSpec(memory_space=pltpu.VMEM),
+        scratch_shapes=[
+            pltpu.VMEM(shape, iterate.dtype),
+            pltpu.VMEM(shape, iterate.dtype),
+            pltpu.SemaphoreType.DMA((n_tensor,)),
+            pltpu.SemaphoreType.DMA((n_tensor,)),
+            pltpu.SemaphoreType.DMA,
+        ],
+        compiler_params=pltpu.CompilerParams(collective_id=1, has_side_effects=True),
+    )(iterate)
+
+
 def on_device(grad, momentum, weight):
     mats, rows_local, cols_local = grad.shape
     n_tensor = lax.axis_size("tensor")
@@ -257,11 +332,10 @@
     def mine(full):
         return lax.dynamic_slice_in_dim(full, start, rows_local, axis=0)
 
-    for step in range(ITERS):
+    for step in range(ITERS - 1):
         gram = jnp.dot(iterate, iterate.T, preferred_element_type=jnp.float32)
-        iterate = polish(iterate, gram, mine if step == ITERS - 1 else None)
-    pieces = iterate.reshape(rows_local, n_tensor, cols_local).transpose(1, 0, 2)
-    ortho = scatter(pieces)
+        iterate = polish(iterate, gram)
+    ortho = finish(iterate, sizes, n_tensor, rows_local)
     width = cols_local * n_tensor
     update = update_gain * math.sqrt(width) * ortho.astype(jnp.float32)
     new_weight = weight - learn_rate * (update + weight_decay * weight)

time: 63.5 us -> 63 us (level)
  matrix products: 8.38 us -> 7.26 us
  Pallas kernels: 47.8 us -> 48.5 us
    dot_general x3 -> x2, matrix products: 2.23 us -> 1.49 us  [on_device(): gram = jnp.dot(iterate, iterate.T, preferred_element_type=jnp.float32)]
    pallas_call x1, Pallas kernels: 8.58 us -> 9.22 us  [finish(): pl.pallas_call(functools.partial(finish_kernel, sizes, n_tensor), out_sha...]
    dot_general x3 -> x2, matrix products: 2.61 us -> 2.25 us  [polish(): squared = jnp.dot(squared_rows, gram, precision=lax.Precision.HIGH)]
    dot_general x3 -> x2, matrix products: 3.54 us -> 3.52 us  [split_dot(): jnp.dot(both, jnp.concatenate([rhs, rhs], axis=0), preferred_element_type...]
where the time goes in v10:
time: 63 us; the launch traced here: 62.5 us
  Pallas kernels  48.5 us (77%)
  matrix products  7.26 us (12%)
  other arithmetic  4.18 us (7%)
  between operations  1.39 us (2%)
  local copies, waits for them, and re-layouts  1.19 us (2%)
    pallas_call x1, Pallas kernels, gather3(): pl.pallas_call(functools.partial(gather3_kernel, sizes, n_tensor), out_sh...  39.3 us
    pallas_call x1, Pallas kernels, finish(): pl.pallas_call(functools.partial(finish_kernel, sizes, n_tensor), out_sha...  9.22 us
    dot_general x2, matrix products, split_dot(): jnp.dot(both, jnp.concatenate([rhs, rhs], axis=0), preferred_element_type...  3.52 us
    dot_general x2, matrix products, polish(): squared = jnp.dot(squared_rows, gram, precision=lax.Precision.HIGH)  2.25 us
    dot_general x2, matrix products, on_device(): gram = jnp.dot(iterate, iterate.T, preferred_element_type=jnp.float32)  1.49 us
    convert_element_type x1, other arithmetic, on_device(): iterate = (wide / frob).astype(jnp.bfloat16)  1.43 us
    convert_element_type x1, other arithmetic, on_device(): advance = (grad + mu_decay * new_momentum).astype(jnp.bfloat16)  1.4 us
    sub x1, other arithmetic, on_device(): new_weight = weight - learn_rate * (update + weight_decay * weight)  1.35 us

profile of v10, /device:TPU:1, one launch (start us, length us, event | category | flops | bytes accessed | tf_op | source)
XLA Modules:
  0.0 62.5 jit_solution(348336549346041495)
XLA Ops:
  0.6 1.4 %add_convert_fusion.2 = (bf16[8,8,128]{2,1,0:T(8,128)(2,1)}, f32[8,8,128]{2,1,0:T(8,128)}) fusion(f32[8,8,128]{2,1,0:T(8,128)} %param.3, f32[8,8,128]{2,1,0:T(8,128)} %param.4), kind=kLoop, calls=%fused_computation.25 | loop fusion | flops 40960 | bytes 114688 | tf_op jit(solution)/shard_map/convert_element_type | solution.py:321
  2.0 39.3 %shard_map.58 = (bf16[512,1024]{1,0:T(8,128)(2,1)}, f32[8,128]{1,0:T(8,128)}) custom-call(bf16[8,8,128]{2,1,0:T(8,128)(2,1)} %get-tuple-element.13.adv_ref), custom_call_target="tpu_custom_call" | custom-call | tf_op jit(solution)/shard_map/pallas_call | solution.py:158
  41.3 1.2 %slice.3 = f32[1,1]{1,0:T(1,128)} slice(f32[8,128]{1,0:T(8,128)} %get-tuple-element.6), slice={[0:1], [0:1]} | slice | bytes 8 | tf_op jit(solution)/shard_map/slice | solution.py:325
  43.2 1.4 %divide_convert_fusion = bf16[512,1024]{1,0:T(8,128)(2,1)S(1)} fusion(bf16[512,1024]{1,0:T(8,128)(2,1)} %get-tuple-element.5, f32[]{:T(128)} %bitcast), kind=kLoop, calls=%fused_computation.10 | loop fusion | flops 1572864 | bytes 2097156 | tf_op jit(solution)/shard_map/convert_element_type | solution.py:326
  44.6 0.7 %fusion.22 = f32[512,512]{0,1:T(8,128)S(1)} fusion(bf16[512,1024]{1,0:T(8,128)(2,1)S(1)} %divide_convert_fusion), kind=kOutput, calls=%fused_computation.29 | convolution fusion | flops 536870912 | bytes 2097152 | tf_op jit(solution)/shard_map/dot_general | solution.py:336
  45.4 1.1 %subtract_convert_fusion.1 = (bf16[512,512]{0,1:T(8,128)(2,1)S(1)}, bf16[512,512]{0,1:T(8,128)(2,1)S(1)}) fusion(f32[512,512]{0,1:T(8,128)S(1)} %fusion.22), kind=kOutput, calls=%fused_computation.22 | convolution fusion | flops 807141376 | bytes 2097152 | tf_op jit(solution)/shard_map/dot_general | solution.py:235
  46.5 1.3 %add_convert_fusion.1 = bf16[512,1024]{1,0:T(8,128)(2,1)S(1)} fusion(bf16[512,1024]{1,0:T(8,128)(2,1)S(1)} %divide_convert_fusion, bf16[512,512]{0,1:T(8,128)(2,1)S(1)} %get-tuple-element.11, bf16[512,512]{0,1:T(8,128)(2,1)S(1)} %get-tuple-element.12), kind=kOutput, calls=%fused_computation.9 | convolution fusion | flops 1082130432 | bytes 3145728 | tf_op jit(solution)/shard_map/dot_general | solution.py:230
  47.8 0.7 %fusion.23 = f32[512,512]{0,1:T(8,128)S(1)} fusion(bf16[512,1024]{1,0:T(8,128)(2,1)S(1)} %add_convert_fusion.1), kind=kOutput, calls=%fused_computation.30 | convolution fusion | flops 536870912 | bytes 2097152 | tf_op jit(solution)/shard_map/dot_general | solution.py:336
  48.5 1.1 %subtract_convert_fusion = (bf16[512,512]{0,1:T(8,128)(2,1)S(1)}, bf16[512,512]{0,1:T(8,128)(2,1)S(1)}) fusion(f32[512,512]{0,1:T(8,128)S(1)} %fusion.23), kind=kOutput, calls=%fused_computation.21 | convolution fusion | flops 807141376 | bytes 2097152 | tf_op jit(solution)/shard_map/dot_general | solution.py:235
  49.7 2.2 %add_convert_fusion.x_ref = bf16[512,1024]{1,0:T(8,128)(2,1)} fusion(bf16[512,1024]{1,0:T(8,128)(2,1)S(1)} %add_convert_fusion.1, bf16[512,512]{0,1:T(8,128)(2,1)S(1)} %get-tuple-element.9, bf16[512,512]{0,1:T(8,128)(2,1)S(1)} %get-tuple-element.10), kind=kOutput, calls=%fused_computation.8 | convolution fusion | flops 1082130432 | bytes 3145728 | tf_op jit(solution)/shard_map/dot_general | solution.py:230
  51.9 0.0 copy-start
  51.9 9.2 %shard_map.59 = bf16[8,8,128]{2,1,0:T(8,128)(2,1)} custom-call(bf16[512,1024]{1,0:T(8,128)(2,1)} %add_convert_fusion.x_ref), custom_call_target="tpu_custom_call" | custom-call | tf_op jit(solution)/shard_map/pallas_call | solution.py:301
  61.1 0.0 copy-done
  61.1 1.4 %multiply_subtract_fusion = (f32[8,8,128]{2,1,0:T(8,128)}, f32[8,8,128]{2,1,0:T(8,128)}) fusion(f32[8,8,128]{2,1,0:T(8,128)S(1)} %copy-done, bf16[8,8,128]{2,1,0:T(8,128)(2,1)} %shard_map.59), kind=kLoop, calls=%fused_computation.23 | loop fusion | flops 49152 | bytes 114688 | tf_op jit(solution)/shard_map/sub | solution.py:341
Async XLA Ops:
  51.9 9.2 %copy-start = (f32[8,8,128]{2,1,0:T(8,128)S(1)}, f32[8,8,128]{2,1,0:T(8,128)}, u32[]{:S(2)}) copy-start(f32[8,8,128]{2,1,0:T(8,128)} %param.5) | copy-start | bytes 98308
